TPU v7x, 32 devices: a whole 2x2x4 slice. The times are simulated.
32 devices in a mesh: seq: 8 (over z, y), tp: 4 (over x, core).
Axes of the slice: x: 2, y: 2, z: 4, core: 2. Of those that a mesh axis runs over, the one named last changes fastest.
Arguments:
- attention_output: bfloat16 [6144, 4096], P('seq', 'tp'), may hold values from -6 to 6
- output_gradient: bfloat16 [6144, 4096], P('seq', 'tp'), may hold values from -6 to 6
- output_weight: bfloat16 [4096, 4096], P('tp'), may hold values from -0.09375 to 0.09375
- adapter_down: bfloat16 [32, 64, 4096], P('seq', None, 'tp'), may hold values from -0.09375 to 0.09375
- adapter_up: bfloat16 [32, 64, 4096], P('seq', None, 'tp'), may hold values from -0.75 to 0.75
- momentum_down: float32 [32, 64, 4096], P('seq', None, 'tp'), may hold values from -6 to 6
- momentum_up: float32 [32, 64, 4096], P('seq', None, 'tp'), may hold values from -6 to 6
- tenant_storage_row: int32 [32], replicated, may hold values from 0 to 31, as said below
- slot_tenant_index: int32 [8, 4], replicated, may hold values from 0 to 31, as said below
- slot_token_rows: int32 [8, 4], replicated, may hold values from 1 to 288, 768 in all within a row
Outputs:
- out_act: bfloat16 [6144, 4096], P('seq', 'tp')
- in_grad: bfloat16 [6144, 4096], P('seq', 'tp')
- step_down: float32 [32, 64, 4096], P('seq', None, 'tp')
- step_up: float32 [32, 64, 4096], P('seq', None, 'tp')
- new_moment_down: float32 [32, 64, 4096], P('seq', None, 'tp')
- new_moment_up: float32 [32, 64, 4096], P('seq', None, 'tp')
Inputs may be any that keep to these rules, and one draw needn't show every extreme that they name: A permutation: tenant t's adapters and momenta are row tenant_storage_row[t], owned by seq index tenant_storage_row[t] // 4. `slot_tenant_index`: the 4 tenants of one seq index have distinct owners; a tenant may stand on several seq indices or on none. `slot_token_rows`: each row sums to 768.
All inputs are finite; a program needn't handle non-finite values.
Results may differ from a plain program's by a relative error of at most 0.014.
Values may be sent and summed in bfloat16 or wider, within the bound.
A program may use at most 128 MiB of HBM per device.

v0:
```python
import jax
import jax.numpy as jnp
from jax import lax
from jax.sharding import PartitionSpec as P

adapter_scale = 2.0
beta_first = 0.9
beta_second = 0.99
soft_floor = 0.25
epsilon = 1e-06


def slot_positions(tenant_storage_row, slot_tenant_index):
    tenant_ids = jnp.arange(tenant_storage_row.shape[0], dtype=jnp.int32)
    match = slot_tenant_index[:, :, None] == tenant_ids[None, None, :]
    return jnp.sum(jnp.where(match, tenant_storage_row[None, None, :], 0), axis=2)


def row_members(counts, row_count):
    ends = jnp.cumsum(counts)
    starts = ends - counts
    index = jnp.arange(row_count, dtype=jnp.int32)
    return (index[:, None] >= starts[None, :]) & (index[:, None] < ends[None, :])


def lion_step(moment, grad):
    combined = beta_first * moment + (1.0 - beta_first) * grad
    spread = jnp.sqrt(jnp.mean(combined * combined, axis=1, keepdims=True) + epsilon)
    step = combined / (jnp.abs(combined) + soft_floor * spread)
    return (step, beta_second * moment + (1.0 - beta_second) * grad)


def local(
    attention_output,
    output_gradient,
    output_weight,
    adapter_down,
    adapter_up,
    momentum_down,
    momentum_up,
    tenant_storage_row,
    slot_tenant_index,
    slot_token_rows,
):
    device = lax.axis_index("seq")
    seq_count = lax.axis_size("seq")
    row_count = attention_output.shape[0]
    slot_count = slot_tenant_index.shape[1]
    adapter_rank_size = adapter_down.shape[1]
    owned_tenant_count = adapter_down.shape[0]
    width_in = attention_output.shape[1]
    width_out = output_gradient.shape[1]
    contract_last = (((1,), (1,)), ((), ()))
    contract_leading = (((0,), (0,)), ((), ()))
    slot_location = slot_positions(tenant_storage_row, slot_tenant_index)
    owner = slot_location // owned_tenant_count
    within = slot_location % owned_tenant_count
    my_position = lax.dynamic_index_in_dim(slot_location, device, 0, keepdims=False)
    my_owner = my_position // owned_tenant_count
    counts = lax.dynamic_index_in_dim(slot_token_rows, device, 0, keepdims=False)
    tenant_mask = row_members(counts, row_count)[:, :, None]
    owned_ids = jnp.arange(owned_tenant_count, dtype=jnp.int32)
    here = (owner == device)[:, :, None] & (within[:, :, None] == owned_ids[None, None, :])
    choose = jnp.sum(here.astype(jnp.float32), axis=1).astype(jnp.bfloat16)
    pieces = (
        lax.all_gather(adapter_down, "seq", axis=0, tiled=True),
        lax.all_gather(adapter_up, "seq", axis=0, tiled=True),
    )
    count = pieces[0].shape[0]
    select = (my_position[:, None] == jnp.arange(count, dtype=jnp.int32)[None, :]).astype(
        jnp.bfloat16
    )
    found_down = jnp.einsum("sp,prd->srd", select, pieces[0], preferred_element_type=jnp.float32)
    found_up = jnp.einsum("sp,prd->srd", select, pieces[1], preferred_element_type=jnp.float32)
    down_tiles_list = found_down.astype(jnp.bfloat16)
    up_tiles_list = found_up.astype(jnp.bfloat16)
    flat_down = down_tiles_list.reshape(slot_count * adapter_rank_size, width_in)
    flattened_up = up_tiles_list.reshape(slot_count * adapter_rank_size, width_out)
    project = lax.dot_general(
        attention_output, flat_down, contract_last, preferred_element_type=jnp.float32
    )
    low_part = jnp.sum(
        jnp.where(tenant_mask, project.reshape(row_count, slot_count, adapter_rank_size), 0.0),
        axis=1,
    )
    backward_pass = lax.dot_general(
        output_gradient, flattened_up, contract_last, preferred_element_type=jnp.float32
    )
    grad_part = jnp.sum(
        jnp.where(
            tenant_mask, backward_pass.reshape(row_count, slot_count, adapter_rank_size), 0.0
        ),
        axis=1,
    )
    low_sum, gradient_total = (
        lax.psum(low_part.astype(jnp.bfloat16), "tp").astype(jnp.float32),
        lax.psum(grad_part.astype(jnp.bfloat16), "tp").astype(jnp.float32),
    )
    low = low_sum.astype(jnp.bfloat16)
    lowrank_gradient = (adapter_scale * gradient_total).astype(jnp.bfloat16)
    spread_lowrank = jnp.where(tenant_mask, low[:, None, :], jnp.zeros((), jnp.bfloat16)).reshape(
        row_count, slot_count * adapter_rank_size
    )
    spread_grad = jnp.where(
        tenant_mask, lowrank_gradient[:, None, :], jnp.zeros((), jnp.bfloat16)
    ).reshape(row_count, slot_count * adapter_rank_size)
    base_terms = jnp.dot(attention_output, output_weight, preferred_element_type=jnp.float32)
    base_output = lax.psum_scatter(
        base_terms.astype(jnp.bfloat16), "tp", scatter_dimension=1, tiled=True
    ).astype(jnp.float32)
    out_act = (
        base_output
        + adapter_scale * jnp.dot(spread_lowrank, flattened_up, preferred_element_type=jnp.float32)
    ).astype(jnp.bfloat16)
    back_base = lax.dot_general(
        lax.all_gather(output_gradient, "tp", axis=1, tiled=True),
        output_weight,
        contract_last,
        preferred_element_type=jnp.float32,
    )
    in_grad = (
        back_base + jnp.dot(spread_grad, flat_down, preferred_element_type=jnp.float32)
    ).astype(jnp.bfloat16)
    part_down = lax.dot_general(
        spread_grad, attention_output, contract_leading, preferred_element_type=jnp.float32
    ).astype(jnp.bfloat16)
    partial_up = (
        adapter_scale
        * lax.dot_general(
            spread_lowrank, output_gradient, contract_leading, preferred_element_type=jnp.float32
        )
    ).astype(jnp.bfloat16)
    to_owner = (jnp.arange(seq_count, dtype=jnp.int32)[:, None] == my_owner[None, :]).astype(
        jnp.bfloat16
    )
    outgoing_down = jnp.einsum(
        "is,srd->ird",
        to_owner,
        part_down.reshape(slot_count, adapter_rank_size, width_in),
        preferred_element_type=jnp.float32,
    ).astype(jnp.bfloat16)
    outgoing_up = jnp.einsum(
        "is,srd->ird",
        to_owner,
        partial_up.reshape(slot_count, adapter_rank_size, width_out),
        preferred_element_type=jnp.float32,
    ).astype(jnp.bfloat16)
    incoming_down, incoming_up = (
        lax.all_to_all(outgoing_down, "seq", split_axis=0, concat_axis=0, tiled=True),
        lax.all_to_all(outgoing_up, "seq", split_axis=0, concat_axis=0, tiled=True),
    )
    total_down = jnp.einsum(
        "ik,ird->krd", choose, incoming_down, preferred_element_type=jnp.float32
    )
    total_up = jnp.einsum("ik,ird->krd", choose, incoming_up, preferred_element_type=jnp.float32)
    my_rows = device * owned_tenant_count + owned_ids
    tokens_here = jnp.sum(
        jnp.where(
            slot_location[:, :, None] == my_rows[None, None, :], slot_token_rows[:, :, None], 0
        ),
        axis=(0, 1),
    )
    denom = jnp.maximum(tokens_here, 1).astype(jnp.float32)
    step_down, new_moment_down = lion_step(momentum_down, total_down / denom[:, None, None])
    step_up, new_moment_up = lion_step(momentum_up, total_up / denom[:, None, None])
    return (out_act, in_grad, step_down, step_up, new_moment_down, new_moment_up)


def solution(mesh):
    return jax.shard_map(
        local,
        mesh=mesh,
        in_specs=(
            P("seq", "tp"),
            P("seq", "tp"),
            P("tp", None),
            P("seq", None, "tp"),
            P("seq", None, "tp"),
            P("seq", None, "tp"),
            P("seq", None, "tp"),
            P(),
            P(),
            P(),
        ),
        out_specs=(
            P("seq", "tp"),
            P("seq", "tp"),
            P("seq", None, "tp"),
            P("seq", None, "tp"),
            P("seq", None, "tp"),
            P("seq", None, "tp"),
        ),
        check_vma=False,
    )
```

profile of v0, /device:TPU:0, one launch (start us, length us, event | category | flops | bytes accessed | tf_op | source)
XLA Modules:
  0.0 318.0 jit_solution(3423727163977238137)
XLA Ops:
  8.0 0.7 all-gather.4.cloned.1.call-update
  8.7 0.8 constant_dynamic-slice_fusion
  9.7 0.9 select_reduce_fusion.2
  10.9 75.3 %all-gather.6.cloned.1.call-done = bf16[32,64,1024]{2,1,0:T(8,128)(2,1)} async-done(((bf16[4,64,1024]{2,1,0:T(8,128)(2,1)}), bf16[32,64,1024]{2,1,0:T(8,128)(2,1)}) %all-gather.6.cloned.1.call-update) | async-done | bytes 4194320 | tf_op jit(solution)/shard_map/all_gather | solution.py:67
  86.3 6.8 %fusion.11 = bf16[4,64,1024]{2,0,1:T(4,128)(2,1)S(1)} fusion(bf16[32,64,1024]{2,1,0:T(8,128)(2,1)} %all-gather.6.cloned.1.call-done, s32[4]{0:T(128)S(1)} %get-tuple-element.39), kind=kOutput, calls=%fused_computation.17 | convolution fusion | flops 17039488 | bytes 4718608 | tf_op jit(solution)/shard_map/sp,prd->srd/dot_general | solution.py:74
  93.1 0.8 copy-done.3
  93.8 1.0 copy.96
  94.8 65.3 %all-gather.4.cloned.1.call-done = bf16[32,64,1024]{2,1,0:T(8,128)(2,1)} async-done(((bf16[4,64,1024]{2,1,0:T(8,128)(2,1)}), bf16[32,64,1024]{2,1,0:T(8,128)(2,1)}) %all-gather.4.cloned.1.call-update) | async-done | bytes 4194320 | tf_op jit(solution)/shard_map/all_gather | solution.py:66
  160.1 6.8 %fusion.8 = bf16[4,64,1024]{2,0,1:T(4,128)(2,1)S(1)} fusion(bf16[32,64,1024]{2,1,0:T(8,128)(2,1)} %all-gather.4.cloned.1.call-done, s32[4]{0:T(128)S(1)} %get-tuple-element.39), kind=kOutput, calls=%fused_computation.16 | convolution fusion | flops 17039488 | bytes 4718608 | tf_op jit(solution)/shard_map/sp,prd->srd/dot_general | solution.py:73
  168.4 0.8 select_reduce_fusion
  170.0 11.9 %convolution_convert_fusion = bf16[768,4096]{1,0:T(8,128)(2,1)} fusion(bf16[768,1024]{1,0:T(8,128)(2,1)S(1)} %copy-done, bf16[1024,4096]{1,0:T(8,128)(2,1)} %param.12), kind=kOutput, calls=%fused_computation | convolution fusion | flops 6445596672 | bytes 16252928 | tf_op jit(solution)/shard_map/dot_general | solution.py:107
  182.0 17.5 %all-reduce.3.cloned.1.call-done = (bf16[768,64]{0,1:T(8,128)(2,1)}, bf16[768,64]{0,1:T(8,128)(2,1)}) async-done(((bf16[768,64]{0,1:T(8,128)(2,1)}, bf16[768,64]{0,1:T(8,128)(2,1)}), (bf16[768,64]{0,1:T(8,128)(2,1)}, bf16[768,64]{0,1:T(8,128)(2,1)})) %all-reduce.3.cloned.1.call-update) | async-done | bytes 196624 | tf_op jit(solution)/shard_map/psum | solution.py:96
  199.4 0.9 multiply_convert_fusion
  200.3 1.0 broadcast_select_fusion.1
  202.6 1.5 copy.101
  204.1 5.5 %all-to-all-start = ((bf16[8,64,1024]{2,1,0:T(8,128)(2,1)}), bf16[8,64,1024]{2,1,0:T(8,128)(2,1)}, u32[]{:S(2)}, u32[]{:S(2)}) async-start(bf16[8,64,1024]{2,1,0:T(8,128)(2,1)} %copy.101), calls=%async_computation.1 | async-start | bytes 2097152 | tf_op jit(solution)/shard_map/all_to_all | solution.py:149
  210.9 1.5 copy.105
  212.5 22.2 %all-to-all-done = bf16[8,64,1024]{2,1,0:T(8,128)(2,1)} async-done(((bf16[8,64,1024]{2,1,0:T(8,128)(2,1)}), bf16[8,64,1024]{2,1,0:T(8,128)(2,1)}, u32[]{:S(2)}, u32[]{:S(2)}) %all-to-all-start) | async-done | bytes 1048608 | tf_op jit(solution)/shard_map/all_to_all | solution.py:149
  234.7 4.2 %all-to-all-start.1 = ((bf16[8,64,1024]{2,1,0:T(8,128)(2,1)}), bf16[8,64,1024]{2,1,0:T(8,128)(2,1)}, u32[]{:S(2)}, u32[]{:S(2)}) async-start(bf16[8,64,1024]{2,1,0:T(8,128)(2,1)} %copy.105), calls=%async_computation.2 | async-start | bytes 2097152 | tf_op jit(solution)/shard_map/all_to_all | solution.py:150
  239.2 4.0 %multiply_add_fusion.1 = (f32[4,64,1024]{2,0,1:T(4,128)}, f32[4,1024]{1,0:T(4,128)S(1)}, f32[4,64,1024]{2,0,1:T(4,128)S(1)}) fusion(f32[4,64,1024]{2,1,0:T(8,128)S(1)} %copy-done.8, f32[4]{0:T(128)S(1)} %maximum_convert_fusion, bf16[8,64,1024]{2,1,0:T(8,128)(2,1)} %all-to-all-done, bf16[8,4]{0,1:T(4,128)(2,1)S(1)} %convert_reduce_fusion), kind=kOutput, calls=%fused_computation.22 | convolution fusion | flops 6549504 | bytes 4210768 | tf_op jit(solution)/shard_map/ik,ird->krd/dot_general | solution.py:152
  243.3 1.2 add_divide_fusion.1
  244.4 1.6 copy.109
  246.0 18.4 %all-to-all-done.1 = bf16[8,64,1024]{2,1,0:T(8,128)(2,1)} async-done(((bf16[8,64,1024]{2,1,0:T(8,128)(2,1)}), bf16[8,64,1024]{2,1,0:T(8,128)(2,1)}, u32[]{:S(2)}, u32[]{:S(2)}) %all-to-all-start.1) | async-done | bytes 1048608 | tf_op jit(solution)/shard_map/all_to_all | solution.py:150
  264.4 3.4 %multiply_add_fusion = (f32[4,64,1024]{2,0,1:T(4,128)S(1)}, f32[4,1024]{1,0:T(4,128)S(1)}, f32[4,64,1024]{2,0,1:T(4,128)S(1)}) fusion(f32[4,64,1024]{2,1,0:T(8,128)} %param.16, f32[4]{0:T(128)S(1)} %maximum_convert_fusion, bf16[8,64,1024]{2,1,0:T(8,128)(2,1)} %all-to-all-done.1, bf16[8,4]{0,1:T(4,128)(2,1)S(1)} %convert_reduce_fusion), kind=kOutput, calls=%fused_computation.21 | convolution fusion | flops 6549504 | bytes 4210768 | tf_op jit(solution)/shard_map/ik,ird->krd/dot_general | solution.py:155
  267.8 1.2 add_divide_fusion
  269.0 1.6 copy.110
  270.6 1.6 copy.111
  272.2 1.6 copy.112
  273.8 11.2 %fusion.45 = f32[768,1024]{1,0:T(8,128)S(1)} fusion(bf16[768,4096]{1,0:T(8,128)(2,1)} %all-gather.8.cloned.1.call-done, bf16[1024,4096]{1,0:T(8,128)(2,1)} %param.12), kind=kOutput, calls=%fused_computation.87 | convolution fusion | flops 6442450944 | bytes 17825792 | tf_op jit(solution)/shard_map/dot_general | solution.py:115
  285.0 1.8 fusion.4
  286.8 21.5 %reduce-scatter.2.cloned.1.call-done = bf16[768,1024]{1,0:T(8,128)(2,1)} async-done(((bf16[768,4096]{1,0:T(8,128)(2,1)}), bf16[768,1024]{1,0:T(8,128)(2,1)}) %reduce-scatter.2.cloned.1.call-update) | async-done | bytes 1572880 | tf_op jit(solution)/shard_map/reduce_scatter | solution.py:108
  308.3 3.2 %fusion.6 = bf16[768,1024]{1,0:T(8,128)(2,1)} fusion(bf16[768,1024]{1,0:T(8,128)(2,1)} %reduce-scatter.2.cloned.1.call-done, pred[768,4]{0,1:T(4,128)(4,1)S(1)} %fusion.18, bf16[768,64]{0,1:T(8,128)(2,1)S(1)} %copy-done.13, bf16[4,64,1024]{2,0,1:T(4,128)(2,1)S(1)} %copy-done.4), kind=kOutput, calls=%fused_computation.9 | convolution fusion | flops 405995520 | bytes 3771392 | tf_op jit(solution)/shard_map/dot_general | solution.py:113
  (59 shorter events, 6.3 us)
Async XLA Ops:
  7.2 160.6 %copy-start = (bf16[768,1024]{1,0:T(8,128)(2,1)S(1)}, bf16[768,1024]{1,0:T(8,128)(2,1)}, u32[]{:S(2)}) copy-start(bf16[768,1024]{1,0:T(8,128)(2,1)} %param.10) | copy-start | bytes 4718596
  7.2 79.1 %all-gather.6.cloned.1.call-start = ((), (), s32[]{:S(2)}) async-start(), calls=%async_computation.5 | async-start | bytes 4718592 | tf_op jit(solution)/shard_map/all_gather | solution.py:67
  7.9 152.2 %all-gather.4.cloned.1.call-start = ((), (), s32[]{:S(2)}) async-start(), calls=%async_computation.4 | async-start | bytes 4718592 | tf_op jit(solution)/shard_map/all_gather | solution.py:66
  8.7 190.8 %all-reduce.3.cloned.1.call-start = ((), (), s32[]{:S(2)}) async-start(), calls=%async_computation.7 | async-start | bytes 393216 | tf_op jit(solution)/shard_map/psum | solution.py:96
  93.1 0.8 copy-start.3
  94.8 72.3 %copy-start.1 = (bf16[768,1024]{1,0:T(8,128)(2,1)S(1)}, bf16[768,1024]{1,0:T(8,128)(2,1)}, u32[]{:S(2)}) copy-start(bf16[768,1024]{1,0:T(8,128)(2,1)} %param.11) | copy-start | bytes 4718596
  160.1 7.0 %copy-start.7 = (bf16[4,64,1024]{2,1,0:T(8,128)(2,1)S(1)}, bf16[4,64,1024]{2,1,0:T(8,128)(2,1)}, u32[]{:S(2)}) copy-start(bf16[4,64,1024]{2,1,0:T(8,128)(2,1)} %copy.96) | copy-start | bytes 1572868
  166.9 1.4 copy-start.5
  169.2 104.6 %all-gather.8.cloned.1.call-start = ((), (), s32[]{:S(2)}) async-start(), calls=%async_computation.6 | async-start | bytes 7864320 | tf_op jit(solution)/shard_map/all_gather | solution.py:116
  169.8 138.5 %reduce-scatter.2.cloned.1.call-start = ((), (), s32[]{:S(2)}) async-start(), calls=%async_computation.3 | async-start | bytes 7864320 | tf_op jit(solution)/shard_map/reduce_scatter | solution.py:108
  200.3 1.6 copy-start.11
  201.9 7.7 %copy-start.2 = (bf16[768,1024]{1,0:T(8,128)(2,1)S(1)}, bf16[768,1024]{1,0:T(8,128)(2,1)}, u32[]{:S(2)}) copy-start(bf16[768,1024]{1,0:T(8,128)(2,1)} %param.11) | copy-start | bytes 4718596
  204.1 30.6 %all-to-all-start = ((bf16[8,64,1024]{2,1,0:T(8,128)(2,1)}), bf16[8,64,1024]{2,1,0:T(8,128)(2,1)}, u32[]{:S(2)}, u32[]{:S(2)}) async-start(bf16[8,64,1024]{2,1,0:T(8,128)(2,1)} %copy.101), calls=%async_computation.1 | async-start | bytes 2097152 | tf_op jit(solution)/shard_map/all_to_all | solution.py:149
  210.3 28.8 %copy-start.14 = (s32[8,4]{0,1:T(4,128)S(1)}, s32[8,4]{0,1:T(4,128)}, u32[]{:S(2)}) copy-start(s32[8,4]{0,1:T(4,128)} %param.19) | copy-start | bytes 388
  210.3 29.0 %copy-start.8 = (f32[4,64,1024]{2,1,0:T(8,128)S(1)}, f32[4,64,1024]{2,1,0:T(8,128)}, u32[]{:S(2)}) copy-start(f32[4,64,1024]{2,1,0:T(8,128)} %param.15) | copy-start | bytes 3145732
  234.7 29.7 %all-to-all-start.1 = ((bf16[8,64,1024]{2,1,0:T(8,128)(2,1)}), bf16[8,64,1024]{2,1,0:T(8,128)(2,1)}, u32[]{:S(2)}, u32[]{:S(2)}) async-start(bf16[8,64,1024]{2,1,0:T(8,128)(2,1)} %copy.105), calls=%async_computation.2 | async-start | bytes 2097152 | tf_op jit(solution)/shard_map/all_to_all | solution.py:150
  246.0 21.8 %copy-start.9 = (f32[4,64,1024]{2,1,0:T(8,128)S(1)}, f32[4,64,1024]{2,1,0:T(8,128)}, u32[]{:S(2)}) copy-start(f32[4,64,1024]{2,1,0:T(8,128)} %param.16) | copy-start | bytes 3145732
  267.8 2.8 copy-start.10
  273.7 11.2 %copy-start.6 = (bf16[4,64,1024]{2,0,1:T(4,128)(2,1)S(1)}, bf16[4,64,1024]{2,0,1:T(4,128)(2,1)}, u32[]{:S(2)}) copy-start(bf16[4,64,1024]{2,0,1:T(4,128)(2,1)} %copy-done.5) | copy-start | bytes 1572868
  273.7 11.2 %copy-start.12 = (bf16[768,64]{0,1:T(8,128)(2,1)S(1)}, bf16[768,64]{0,1:T(8,128)(2,1)}, u32[]{:S(2)}) copy-start(bf16[768,64]{0,1:T(8,128)(2,1)} %copy-done.11) | copy-start | bytes 294916
  285.0 23.3 %copy-start.4 = (bf16[4,64,1024]{2,0,1:T(4,128)(2,1)S(1)}, bf16[4,64,1024]{2,0,1:T(4,128)(2,1)}, u32[]{:S(2)}) copy-start(bf16[4,64,1024]{2,0,1:T(4,128)(2,1)} %copy-done.3) | copy-start | bytes 1572868
  285.0 23.3 %copy-start.13 = (bf16[768,64]{0,1:T(8,128)(2,1)S(1)}, bf16[768,64]{0,1:T(8,128)(2,1)}, u32[]{:S(2)}) copy-start(bf16[768,64]{0,1:T(8,128)(2,1)} %get-tuple-element.40) | copy-start | bytes 294916
Sparse Core Ops, SparseCore 0:
  10.1 76.0 all-gather.5
  88.4 71.6 all-gather.3
  169.3 30.0 all-reduce.2
  200.9 46.3 all-gather.7
  249.9 58.3 reduce-scatter.1
where the time goes:
time: 319 us; the launch traced here: 318 us
  waiting for transfers between devices  222 us (70%)
  matrix products  52.8 us (17%)
  between operations  14.1 us (4%)
  local copies, waits for them, and re-layouts  12.2 us (4%)
  starting transfers between devices  10.1 us (3%)
  other arithmetic  6.68 us (2%)
    all_gather x1, waiting for transfers between devices, local(): lax.all_gather(adapter_up, 'seq', axis=0, tiled=True)  75.3 us
    all_gather x1, waiting for transfers between devices, local(): lax.all_gather(adapter_down, 'seq', axis=0, tiled=True)  65.3 us
    all_to_all x1, waiting for transfers between devices, local(): lax.all_to_all(outgoing_down, 'seq', split_axis=0, concat_axis=0, tiled=T...  22.2 us
    reduce_scatter x1, waiting for transfers between devices, local(): lax.psum_scatter(base_terms.astype(jnp.bfloat16), 'tp', scatter_dimension...  21.5 us
    all_to_all x1, waiting for transfers between devices, local(): lax.all_to_all(outgoing_up, 'seq', split_axis=0, concat_axis=0, tiled=True)  18.4 us
    psum x1, waiting for transfers between devices, local(): lax.psum(low_part.astype(jnp.bfloat16), 'tp').astype(jnp.float32)  17.5 us
    dot_general x1, matrix products, local(): jnp.dot(attention_output, output_weight, preferred_element_type=jnp.float32)  11.9 us
    dot_general x1, matrix products, local(): lax.dot_general(lax.all_gather(output_gradient, 'tp', axis=1, tiled=True)...  11.2 us
  transfers between devices with their start and end apart: 7, of which 6 were waited for; matrix products, arithmetic and copies ran while one was open for 18% of the time, Pallas kernels for 0%

commit v1 on v0

v1 whole, which is shorter than its diff:
```python
import functools

import jax
import jax.numpy as jnp
from jax import lax
from jax.experimental import pallas as pl
from jax.experimental.pallas import tpu as pltpu
from jax.sharding import PartitionSpec as P

adapter_scale = 2.0
beta_first = 0.9
beta_second = 0.99
soft_floor = 0.25
epsilon = 1e-06
contract_last = (((1,), (1,)), ((), ()))
contract_leading = (((0,), (0,)), ((), ()))


def slot_positions(tenant_storage_row, slot_tenant_index):
    tenant_ids = jnp.arange(tenant_storage_row.shape[0], dtype=jnp.int32)
    match = slot_tenant_index[:, :, None] == tenant_ids[None, None, :]
    return jnp.sum(jnp.where(match, tenant_storage_row[None, None, :], 0), axis=2)


def pick_kernel(which_ref, in_ref, out_ref):
    out_ref[...] = in_ref[...]


def pick(which, table):
    count = which.shape[0]
    _, rank, width = table.shape
    return pl.pallas_call(
        pick_kernel,
        out_shape=jax.ShapeDtypeStruct((count, rank, width), table.dtype),
        grid_spec=pltpu.PrefetchScalarGridSpec(
            num_scalar_prefetch=1,
            grid=(count,),
            in_specs=[pl.BlockSpec((1, rank, width), lambda j, which_ref: (which_ref[j], 0, 0))],
            out_specs=pl.BlockSpec((1, rank, width), lambda j, which_ref: (j, 0, 0)),
        ),
        cost_estimate=pl.CostEstimate(
            flops=0, transcendentals=0, bytes_accessed=2 * count * rank * width * 2
        ),
        name="pick",
    )(which, table)


def lion_kernel(seq_count, owned, choose_ref, scale_ref, incoming_ref, moment_ref, step_ref, new_ref):
    for k in range(owned):
        total = None
        for i in range(seq_count):
            term = choose_ref[i * owned + k] * incoming_ref[i].astype(jnp.float32)
            total = term if total is None else total + term
        grad = total / scale_ref[k]
        moment = moment_ref[k]
        combined = beta_first * moment + (1.0 - beta_first) * grad
        spread = jnp.sqrt(jnp.mean(combined * combined, axis=0, keepdims=True) + epsilon)
        step_ref[k] = combined / (jnp.abs(combined) + soft_floor * spread)
        new_ref[k] = beta_second * moment + (1.0 - beta_second) * grad


def lion(choose, denom, incoming, moment):
    seq_count, rank, width = incoming.shape
    owned = moment.shape[0]
    tile = min(256, width)
    block = pl.BlockSpec((owned, rank, tile), lambda j: (0, 0, j))
    shape = jax.ShapeDtypeStruct(moment.shape, jnp.float32)
    smem = pl.BlockSpec(memory_space=pltpu.SMEM)
    return pl.pallas_call(
        functools.partial(lion_kernel, seq_count, owned),
        out_shape=(shape, shape),
        grid=(width // tile,),
        in_specs=[smem, smem, pl.BlockSpec((seq_count, rank, tile), lambda j: (0, 0, j)), block],
        out_specs=(block, block),
        cost_estimate=pl.CostEstimate(
            flops=2 * owned * seq_count * rank * width,
            transcendentals=owned * rank * width,
            bytes_accessed=seq_count * rank * width * 2 + 3 * owned * rank * width * 4,
        ),
        compiler_params=pltpu.CompilerParams(vmem_limit_bytes=32 * 1024 * 1024),
        name="lion",
    )(choose, denom, incoming, moment)


def local(
    attention_output,
    output_gradient,
    output_weight,
    adapter_down,
    adapter_up,
    momentum_down,
    momentum_up,
    tenant_storage_row,
    slot_tenant_index,
    slot_token_rows,
):
    device = lax.axis_index("seq")
    seq_count = lax.axis_size("seq")
    tp_count = lax.axis_size("tp")
    row_count = attention_output.shape[0]
    rank = adapter_down.shape[1]
    owned = adapter_down.shape[0]
    width = attention_output.shape[1]
    slot_location = slot_positions(tenant_storage_row, slot_tenant_index)
    owner = slot_location // owned
    within = slot_location % owned
    owned_ids = jnp.arange(owned, dtype=jnp.int32)
    seq_ids = jnp.arange(seq_count, dtype=jnp.int32)
    mine = owner == device
    send_row = jnp.sum(jnp.where(mine, within, 0), axis=1)
    up_out = pick(send_row, adapter_up)
    down_out = pick(send_row, adapter_down)
    up = lax.all_to_all(up_out, "seq", split_axis=0, concat_axis=0, tiled=True)
    up = up.reshape(seq_count * rank, width)
    down = lax.all_to_all(down_out, "seq", split_axis=0, concat_axis=0, tiled=True)
    down = down.reshape(seq_count * rank, width)

    gathered = lax.all_gather(output_gradient, "tp", axis=1, tiled=True)
    base_terms = jnp.dot(attention_output, output_weight, preferred_element_type=jnp.float32)
    base_output = lax.psum_scatter(
        base_terms.astype(jnp.bfloat16), "tp", scatter_dimension=1, tiled=True
    ).astype(jnp.float32)

    my_owner = lax.dynamic_index_in_dim(owner, device, 0, keepdims=False)
    counts = lax.dynamic_index_in_dim(slot_token_rows, device, 0, keepdims=False)
    slot_ids = jnp.arange(counts.shape[0], dtype=jnp.int32)
    starts = jnp.sum(jnp.where(slot_ids[None, :] < slot_ids[:, None], counts[None, :], 0), axis=1)
    hit = my_owner[None, :] == seq_ids[:, None]
    first = jnp.sum(jnp.where(hit, starts[None, :], 0), axis=1)
    last = jnp.sum(jnp.where(hit, (starts + counts)[None, :], 0), axis=1)
    row_ids = jnp.arange(row_count, dtype=jnp.int32)
    mask = (row_ids[None, :] >= first[:, None]) & (row_ids[None, :] < last[:, None])
    mask = mask[:, None, :]

    def project(blocks, rows):
        product = lax.dot_general(blocks, rows, contract_last, preferred_element_type=jnp.float32)
        part = jnp.sum(jnp.where(mask, product.reshape(seq_count, rank, row_count), 0.0), axis=0)
        part = part.astype(jnp.bfloat16)
        total = part.astype(jnp.float32)
        for k in range(1, tp_count):
            order = [(i, (i + k) % tp_count) for i in range(tp_count)]
            total = total + lax.ppermute(part, "tp", order).astype(jnp.float32)
        return total

    def spread(values):
        wide = jnp.where(mask, values[None], jnp.zeros((), jnp.bfloat16))
        return wide.reshape(seq_count * rank, row_count)

    low_grad = (adapter_scale * project(up, output_gradient)).astype(jnp.bfloat16)
    spread_grad = spread(low_grad)
    part_down = jnp.dot(
        spread_grad, attention_output, preferred_element_type=jnp.float32
    ).astype(jnp.bfloat16)
    incoming_down = lax.all_to_all(
        part_down.reshape(seq_count, rank, width), "seq", split_axis=0, concat_axis=0, tiled=True
    )
    low = project(down, attention_output).astype(jnp.bfloat16)
    spread_low = spread(low)
    part_up = (
        adapter_scale * jnp.dot(spread_low, output_gradient, preferred_element_type=jnp.float32)
    ).astype(jnp.bfloat16)
    incoming_up = lax.all_to_all(
        part_up.reshape(seq_count, rank, width), "seq", split_axis=0, concat_axis=0, tiled=True
    )

    back_base = lax.dot_general(
        gathered, output_weight, contract_last, preferred_element_type=jnp.float32
    )
    in_grad = (
        back_base
        + lax.dot_general(spread_grad, down, contract_leading, preferred_element_type=jnp.float32)
    ).astype(jnp.bfloat16)
    out_act = (
        base_output
        + adapter_scale
        * lax.dot_general(spread_low, up, contract_leading, preferred_element_type=jnp.float32)
    ).astype(jnp.bfloat16)

    here = mine[:, :, None] & (within[:, :, None] == owned_ids[None, None, :])
    choose = jnp.sum(here.astype(jnp.float32), axis=1).reshape(seq_count * owned)
    tokens_here = jnp.sum(jnp.where(here, slot_token_rows[:, :, None], 0), axis=(0, 1))
    denom = jnp.maximum(tokens_here, 1).astype(jnp.float32)
    step_down, new_moment_down = lion(choose, denom, incoming_down, momentum_down)
    step_up, new_moment_up = lion(choose, denom, incoming_up, momentum_up)
    return (out_act, in_grad, step_down, step_up, new_moment_down, new_moment_up)


def solution(mesh):
    return jax.shard_map(
        local,
        mesh=mesh,
        in_specs=(
            P("seq", "tp"),
            P("seq", "tp"),
            P("tp", None),
            P("seq", None, "tp"),
            P("seq", None, "tp"),
            P("seq", None, "tp"),
            P("seq", None, "tp"),
            P(),
            P(),
            P(),
        ),
        out_specs=(
            P("seq", "tp"),
            P("seq", "tp"),
            P("seq", None, "tp"),
            P("seq", None, "tp"),
            P("seq", None, "tp"),
            P("seq", None, "tp"),
        ),
        check_vma=False,
    )
```

time: 319 us -> 195 us (0.61)
  waiting for transfers between devices: 222 us -> 92.3 us
  Pallas kernels: 0 us -> 17.9 us
  matrix products: 52.8 us -> 39 us
  starting transfers between devices: 10.1 us -> 23.2 us
  local copies, waits for them, and re-layouts: 12.2 us -> 4.84 us
  other arithmetic: 6.68 us -> 2.36 us
    all_gather x3 -> x1, waiting for transfers between devices: 141 us -> 0.02 us  [local(): gathered = lax.all_gather(output_gradient, 'tp', axis=1, tiled=True)]
    all_to_all x2 -> x4, waiting for transfers between devices: 40.6 us -> 83.4 us  [the longest x1 21.8 us: local(): lax.all_to_all(part_down.reshape(seq_count, rank, width), 'seq', split_ax...]
    reduce_scatter x1, waiting for transfers between devices: 21.5 us -> 0.01 us  [local(): lax.psum_scatter(base_terms.astype(jnp.bfloat16), 'tp', scatter_dimension...]
    pallas_call x0 -> x4, Pallas kernels: none -> 17.9 us  [the longest x2 10.5 us: pick(): pl.pallas_call(pick_kernel, out_shape=jax.ShapeDtypeStruct((count, rank,...]
    psum x1 -> x0, waiting for transfers between devices: 17.5 us -> none  [local(): lax.psum(low_part.astype(jnp.bfloat16), 'tp').astype(jnp.float32)]
    dot_general x13 -> x7, matrix products: 40.8 us -> 27.1 us  [the longest x1 11.1 us: local(): lax.dot_general(gathered, output_weight, contract_last, preferred_element...]
    all_to_all x2 -> x4, starting transfers between devices: 9.76 us -> 19.5 us  [the longest x1 7.31 us: local(): lax.all_to_all(down_out, 'seq', split_axis=0, concat_axis=0, tiled=True)]
    ppermute x0 -> x6, waiting for transfers between devices: none -> 8.1 us  [project(): total = total + lax.ppermute(part, 'tp', order).astype(jnp.float32)]
  transfers between devices with their start and end apart: 7 -> 12, of which waited for: 6 -> 7; matrix products, arithmetic and copies ran while one was open for 18% -> 20% of each run, Pallas kernels for 0% -> 9%
where the time goes in v1:
time: 195 us; the launch traced here: 194 us
  waiting for transfers between devices  92.3 us (47%)
  matrix products  39 us (20%)
  starting transfers between devices  23.2 us (12%)
  Pallas kernels  17.9 us (9%)
  between operations  14.2 us (7%)
  local copies, waits for them, and re-layouts  4.84 us (2%)
  other arithmetic  2.36 us (1%)
    all_to_all x1, waiting for transfers between devices, local(): lax.all_to_all(part_down.reshape(seq_count, rank, width), 'seq', split_ax...  21.8 us
    all_to_all x1, waiting for transfers between devices, local(): up = lax.all_to_all(up_out, 'seq', split_axis=0, concat_axis=0, tiled=True)  20.8 us
    all_to_all x1, waiting for transfers between devices, local(): lax.all_to_all(down_out, 'seq', split_axis=0, concat_axis=0, tiled=True)  20.5 us
    all_to_all x1, waiting for transfers between devices, local(): lax.all_to_all(part_up.reshape(seq_count, rank, width), 'seq', split_axis...  20.4 us
    dot_general x1, matrix products, local(): jnp.dot(attention_output, output_weight, preferred_element_type=jnp.float32)  11.9 us
    dot_general x1, matrix products, local(): lax.dot_general(gathered, output_weight, contract_last, preferred_element...  11.1 us
    pallas_call x2, Pallas kernels, pick(): pl.pallas_call(pick_kernel, out_shape=jax.ShapeDtypeStruct((count, rank,...  10.5 us
    ppermute x6, waiting for transfers between devices, project(): total = total + lax.ppermute(part, 'tp', order).astype(jnp.float32)  8.1 us
  transfers between devices with their start and end apart: 12, of which 7 were waited for; matrix products, arithmetic and copies ran while one was open for 20% of the time, Pallas kernels for 9%

profile of v1, /device:TPU:0, one launch (start us, length us, event | category | flops | bytes accessed | tf_op | source)
XLA Modules:
  0.0 193.8 jit_solution(6797605828485450280)
XLA Ops:
  7.2 0.7 all-gather.2.cloned.1.call-update
  8.0 0.6 copy-done
  8.6 11.9 %convolution_convert_fusion = bf16[768,4096]{1,0:T(8,128)(2,1)} fusion(bf16[768,1024]{1,0:T(8,128)(2,1)S(1)} %copy-done, bf16[1024,4096]{1,0:T(8,128)(2,1)} %param.12), kind=kOutput, calls=%fused_computation | convolution fusion | flops 6445596672 | bytes 16252928 | tf_op jit(solution)/shard_map/dot_general | solution.py:119
  20.5 0.7 copy-done.10
  21.3 0.5 select_reduce_fusion.4
  21.9 5.2 %pick.2 = bf16[8,64,1024]{2,1,0:T(8,128)(2,1)} custom-call(s32[8]{0:T(128)} %get-tuple-element.16.which_ref, bf16[4,64,1024]{2,1,0:T(8,128)(2,1)} %in_ref.2), custom_call_target="tpu_custom_call" | custom-call | bytes 2097152 | tf_op jit(solution)/shard_map/pick/pallas_call | solution.py:32
  27.1 7.3 %all-to-all-start = ((bf16[8,64,1024]{2,1,0:T(8,128)(2,1)}), bf16[8,64,1024]{2,1,0:T(8,128)(2,1)S(1)}, u32[]{:S(2)}, u32[]{:S(2)}) async-start(bf16[8,64,1024]{2,1,0:T(8,128)(2,1)} %pick.2), calls=%async_computation.1 | async-start | bytes 2097152 | tf_op jit(solution)/shard_map/all_to_all | solution.py:115
  34.4 5.3 %pick.3 = bf16[8,64,1024]{2,1,0:T(8,128)(2,1)} custom-call(s32[8]{0:T(128)} %get-tuple-element.16.which_ref, bf16[4,64,1024]{2,1,0:T(8,128)(2,1)} %in_ref.3), custom_call_target="tpu_custom_call" | custom-call | bytes 2097152 | tf_op jit(solution)/shard_map/pick/pallas_call | solution.py:32
  39.7 20.5 %all-to-all-done = bf16[8,64,1024]{2,1,0:T(8,128)(2,1)S(1)} async-done(((bf16[8,64,1024]{2,1,0:T(8,128)(2,1)}), bf16[8,64,1024]{2,1,0:T(8,128)(2,1)S(1)}, u32[]{:S(2)}, u32[]{:S(2)}) %all-to-all-start) | async-done | bytes 1048608 | tf_op jit(solution)/shard_map/all_to_all | solution.py:115
  60.1 4.2 %all-to-all-start.1 = ((bf16[8,64,1024]{2,1,0:T(8,128)(2,1)}), bf16[8,64,1024]{2,1,0:T(8,128)(2,1)}, u32[]{:S(2)}, u32[]{:S(2)}) async-start(bf16[8,64,1024]{2,1,0:T(8,128)(2,1)} %pick.3), calls=%async_computation.2 | async-start | bytes 2097152 | tf_op jit(solution)/shard_map/all_to_all | solution.py:113
  65.0 2.4 %select_reduce_fusion.1 = bf16[64,768]{1,0:T(8,128)(2,1)S(1)} fusion(bf16[8,64,1024]{2,1,0:T(8,128)(2,1)} %copy-done.4, bf16[768,1024]{1,0:T(8,128)(2,1)S(1)} %copy-done, pred[8,768]{1,0:T(8,128)(4,1)S(1)} %fusion.11), kind=kOutput, calls=%fused_computation.12 | convolution fusion | flops 806043648 | bytes 2725888 | tf_op jit(solution)/shard_map/dot_general | solution.py:136
  67.6 1.4 collective-permute-start.1
  69.2 20.8 %all-to-all-done.1 = bf16[8,64,1024]{2,1,0:T(8,128)(2,1)} async-done(((bf16[8,64,1024]{2,1,0:T(8,128)(2,1)}), bf16[8,64,1024]{2,1,0:T(8,128)(2,1)}, u32[]{:S(2)}, u32[]{:S(2)}) %all-to-all-start.1) | async-done | bytes 1048608 | tf_op jit(solution)/shard_map/all_to_all | solution.py:113
  90.0 2.2 %select_reduce_fusion = bf16[64,768]{1,0:T(8,128)(2,1)S(1)} fusion(bf16[8,64,1024]{2,1,0:T(8,128)(2,1)} %all-to-all-done.1, bf16[768,1024]{1,0:T(8,128)(2,1)S(1)} %copy-done.3, pred[8,768]{1,0:T(8,128)(4,1)S(1)} %fusion.11), kind=kOutput, calls=%fused_computation.11 | convolution fusion | flops 806043648 | bytes 2725888 | tf_op jit(solution)/shard_map/dot_general | solution.py:136
  92.3 1.6 collective-permute-start.4
  94.0 0.6 copy-done.8
  94.7 1.0 add_convert_fusion
  95.7 1.5 collective-permute-done.5
  97.2 6.5 %collective-permute-done.4 = bf16[64,768]{1,0:T(8,128)(2,1)S(1)} collective-permute-done((bf16[64,768]{1,0:T(8,128)(2,1)S(1)}, bf16[64,768]{1,0:T(8,128)(2,1)S(1)}, u32[]{:S(2)}, u32[]{:S(2)}) %collective-permute-start.4) | collective-permute-done | bytes 98336 | tf_op jit(solution)/shard_map/ppermute | solution.py:142
  104.0 2.0 %convolution_convert_fusion.1 = bf16[512,1024]{1,0:T(8,128)(2,1)} fusion(bf16[512,768]{1,0:T(8,128)(2,1)S(1)} %bitcast.46, bf16[768,1024]{1,0:T(8,128)(2,1)S(1)} %copy-done), kind=kOutput, calls=%fused_computation.13 | convolution fusion | flops 805830656 | bytes 3407872 | tf_op jit(solution)/shard_map/dot_general | solution.py:151
  105.9 3.6 %all-to-all-start.2 = ((bf16[8,64,1024]{2,1,0:T(8,128)(2,1)}), bf16[8,64,1024]{2,1,0:T(8,128)(2,1)S(1)}, u32[]{:S(2)}, u32[]{:S(2)}) async-start(bf16[8,64,1024]{2,1,0:T(8,128)(2,1)} %bitcast.44), calls=%async_computation.3 | async-start | bytes 2097152 | tf_op jit(solution)/shard_map/all_to_all | solution.py:154
  109.5 3.4 %multiply_convert_fusion = bf16[512,1024]{1,0:T(8,128)(2,1)} fusion(bf16[512,768]{1,0:T(8,128)(2,1)S(1)} %bitcast.45, bf16[768,1024]{1,0:T(8,128)(2,1)} %param.11), kind=kOutput, calls=%fused_computation.6 | convolution fusion | flops 806354944 | bytes 3407872 | tf_op jit(solution)/shard_map/dot_general | solution.py:160
  112.9 21.8 %all-to-all-done.2.incoming_ref = bf16[8,64,1024]{2,1,0:T(8,128)(2,1)S(1)} async-done(((bf16[8,64,1024]{2,1,0:T(8,128)(2,1)}), bf16[8,64,1024]{2,1,0:T(8,128)(2,1)S(1)}, u32[]{:S(2)}, u32[]{:S(2)}) %all-to-all-start.2) | async-done | bytes 1048608 | tf_op jit(solution)/shard_map/all_to_all | solution.py:154
  134.6 4.4 %all-to-all-start.3 = ((bf16[8,64,1024]{2,1,0:T(8,128)(2,1)}), bf16[8,64,1024]{2,1,0:T(8,128)(2,1)}, u32[]{:S(2)}, u32[]{:S(2)}) async-start(bf16[8,64,1024]{2,1,0:T(8,128)(2,1)} %bitcast.43), calls=%async_computation.4 | async-start | bytes 2097152 | tf_op jit(solution)/shard_map/all_to_all | solution.py:162
  139.4 1.2 copy-done.1
  140.6 3.3 %lion.2 = (f32[4,64,1024]{2,1,0:T(8,128)}, f32[4,64,1024]{2,1,0:T(8,128)}) custom-call(f32[32]{0:T(128)S(1)} %reshape.112.choose_ref, f32[4]{0:T(128)S(1)} %maximum_convert_fusion.scale_ref, bf16[8,64,1024]{2,1,0:T(8,128)(2,1)S(1)} %all-to-all-done.2.incoming_ref, f32[4,64,1024]{2,1,0:T(8,128)S(1)} %copy-done.1), custom_call_target="tpu_custom_call" | custom-call | flops 4194304 | bytes 4194304 | tf_op jit(solution)/shard_map/lion/pallas_call | solution.py:69
  143.9 20.4 %all-to-all-done.3.incoming_ref = bf16[8,64,1024]{2,1,0:T(8,128)(2,1)} async-done(((bf16[8,64,1024]{2,1,0:T(8,128)(2,1)}), bf16[8,64,1024]{2,1,0:T(8,128)(2,1)}, u32[]{:S(2)}, u32[]{:S(2)}) %all-to-all-start.3) | async-done | bytes 1048608 | tf_op jit(solution)/shard_map/all_to_all | solution.py:162
  164.3 1.2 copy-done.2
  165.5 4.2 %lion.3 = (f32[4,64,1024]{2,1,0:T(8,128)}, f32[4,64,1024]{2,1,0:T(8,128)}) custom-call(f32[32]{0:T(128)S(1)} %reshape.112.choose_ref, f32[4]{0:T(128)S(1)} %maximum_convert_fusion.scale_ref, bf16[8,64,1024]{2,1,0:T(8,128)(2,1)} %all-to-all-done.3.incoming_ref, f32[4,64,1024]{2,1,0:T(8,128)S(1)} %copy-done.2), custom_call_target="tpu_custom_call" | custom-call | flops 4194304 | bytes 4194304 | tf_op jit(solution)/shard_map/lion/pallas_call | solution.py:69
  169.7 11.1 %fusion.17 = f32[768,1024]{1,0:T(8,128)S(1)} fusion(bf16[768,4096]{1,0:T(8,128)(2,1)} %all-gather.2.cloned.1.call-done, bf16[1024,4096]{1,0:T(8,128)(2,1)} %param.12), kind=kOutput, calls=%fused_computation.49 | convolution fusion | flops 6442450944 | bytes 17825792 | tf_op jit(solution)/shard_map/dot_general | solution.py:166
  180.8 2.2 %fusion = bf16[768,1024]{1,0:T(8,128)(2,1)} fusion(f32[768,1024]{1,0:T(8,128)S(1)} %fusion.17, bf16[8,64,1024]{2,1,0:T(8,128)(2,1)S(1)} %copy-done.5, pred[8,768]{1,0:T(8,128)(4,1)S(1)} %fusion.11, bf16[64,768]{1,0:T(8,128)(2,1)S(1)} %copy-done.7), kind=kOutput, calls=%fused_computation.2 | convolution fusion | flops 807272448 | bytes 5871616 | tf_op jit(solution)/shard_map/dot_general | solution.py:171
  183.0 3.9 %fusion.2 = bf16[768,1024]{1,0:T(8,128)(2,1)} fusion(bf16[768,1024]{1,0:T(8,128)(2,1)} %reduce-scatter.2.cloned.1.call-done, bf16[8,64,1024]{2,1,0:T(8,128)(2,1)} %all-to-all-done.1, pred[8,768]{1,0:T(8,128)(4,1)S(1)} %fusion.11, bf16[64,768]{1,0:T(8,128)(2,1)S(1)} %add_convert_fusion), kind=kOutput, calls=%fused_computation.5 | convolution fusion | flops 808845312 | bytes 4298752 | tf_op jit(solution)/shard_map/dot_general | solution.py:176
  (46 shorter events, 2.1 us)
Async XLA Ops:
  7.2 1.4 copy-start
  7.2 162.5 %all-gather.2.cloned.1.call-start = ((), (), s32[]{:S(2)}) async-start(), calls=%async_computation.6 | async-start | bytes 7864320 | tf_op jit(solution)/shard_map/all_gather | solution.py:118
  7.9 175.1 %reduce-scatter.2.cloned.1.call-start = ((), (), s32[]{:S(2)}) async-start(), calls=%async_computation.5 | async-start | bytes 7864320 | tf_op jit(solution)/shard_map/reduce_scatter | solution.py:120
  20.4 0.7 copy-start.10
  20.4 0.7 copy-start.11
  27.1 33.1 %all-to-all-start = ((bf16[8,64,1024]{2,1,0:T(8,128)(2,1)}), bf16[8,64,1024]{2,1,0:T(8,128)(2,1)S(1)}, u32[]{:S(2)}, u32[]{:S(2)}) async-start(bf16[8,64,1024]{2,1,0:T(8,128)(2,1)} %pick.2), calls=%async_computation.1 | async-start | bytes 2097152 | tf_op jit(solution)/shard_map/all_to_all | solution.py:115
  34.4 30.0 %copy-start.9 = (s32[8,4]{0,1:T(4,128)S(1)}, s32[8,4]{0,1:T(4,128)}, u32[]{:S(2)}) copy-start(s32[8,4]{0,1:T(4,128)} %param.19) | copy-start | bytes 388
  60.1 4.8 %copy-start.4 = (bf16[8,64,1024]{2,1,0:T(8,128)(2,1)}, bf16[8,64,1024]{2,1,0:T(8,128)(2,1)S(1)}, u32[]{:S(2)}) copy-start(bf16[8,64,1024]{2,1,0:T(8,128)(2,1)S(1)} %all-to-all-done) | copy-start | bytes 3145732
  60.1 29.8 %all-to-all-start.1 = ((bf16[8,64,1024]{2,1,0:T(8,128)(2,1)}), bf16[8,64,1024]{2,1,0:T(8,128)(2,1)}, u32[]{:S(2)}, u32[]{:S(2)}) async-start(bf16[8,64,1024]{2,1,0:T(8,128)(2,1)} %pick.3), calls=%async_computation.2 | async-start | bytes 2097152 | tf_op jit(solution)/shard_map/all_to_all | solution.py:113
  65.0 25.0 %copy-start.3 = (bf16[768,1024]{1,0:T(8,128)(2,1)S(1)}, bf16[768,1024]{1,0:T(8,128)(2,1)}, u32[]{:S(2)}) copy-start(bf16[768,1024]{1,0:T(8,128)(2,1)} %param.11) | copy-start | bytes 4718596
  67.4 26.5 %collective-permute-start.2 = (bf16[64,768]{1,0:T(8,128)(2,1)S(1)}, bf16[64,768]{1,0:T(8,128)(2,1)S(1)}, u32[]{:S(2)}, u32[]{:S(2)}) collective-permute-start(bf16[64,768]{1,0:T(8,128)(2,1)S(1)} %select_reduce_fusion.1), channel_id=1, source_target_pairs={{0,3},{1,0},{2,1},{3,2},{4,7},{5,4},{6,5},{7,6},{8,11},{9,8},{10,9... | collective-permute-start | bytes 294920 | tf_op jit(solution)/shard_map/ppermute | solution.py:142
  67.6 26.5 %collective-permute-start.1 = (bf16[64,768]{1,0:T(8,128)(2,1)S(1)}, bf16[64,768]{1,0:T(8,128)(2,1)S(1)}, u32[]{:S(2)}, u32[]{:S(2)}) collective-permute-start(bf16[64,768]{1,0:T(8,128)(2,1)S(1)} %select_reduce_fusion.1), channel_id=1, source_target_pairs={{0,2},{1,3},{2,0},{3,1},{4,6},{5,7},{6,4},{7,5},{8,10},{9,11},{10,... | collective-permute-start | bytes 294920 | tf_op jit(solution)/shard_map/ppermute | solution.py:142
  69.0 25.7 %collective-permute-start = (bf16[64,768]{1,0:T(8,128)(2,1)S(1)}, bf16[64,768]{1,0:T(8,128)(2,1)}, u32[]{:S(2)}, u32[]{:S(2)}) collective-permute-start(bf16[64,768]{1,0:T(8,128)(2,1)S(1)} %select_reduce_fusion.1), channel_id=1, source_target_pairs={{0,1},{1,2},{2,3},{3,0},{4,5},{5,6},{6,7},{7,4},{8,9},{9,10},{10,1... | collective-permute-start | bytes 294920 | tf_op jit(solution)/shard_map/ppermute | solution.py:142
  92.3 5.0 %collective-permute-start.5 = (bf16[64,768]{1,0:T(8,128)(2,1)S(1)}, bf16[64,768]{1,0:T(8,128)(2,1)S(1)}, u32[]{:S(2)}, u32[]{:S(2)}) collective-permute-start(bf16[64,768]{1,0:T(8,128)(2,1)S(1)} %select_reduce_fusion), channel_id=1, source_target_pairs={{0,3},{1,0},{2,1},{3,2},{4,7},{5,4},{6,5},{7,6},{8,11},{9,8},{10,9... | collective-permute-start | bytes 294920 | tf_op jit(solution)/shard_map/ppermute | solution.py:142
  92.3 11.4 %collective-permute-start.4 = (bf16[64,768]{1,0:T(8,128)(2,1)S(1)}, bf16[64,768]{1,0:T(8,128)(2,1)S(1)}, u32[]{:S(2)}, u32[]{:S(2)}) collective-permute-start(bf16[64,768]{1,0:T(8,128)(2,1)S(1)} %select_reduce_fusion), channel_id=1, source_target_pairs={{0,2},{1,3},{2,0},{3,1},{4,6},{5,7},{6,4},{7,5},{8,10},{9,11},{10,... | collective-permute-start | bytes 294920 | tf_op jit(solution)/shard_map/ppermute | solution.py:142
  93.9 9.9 %collective-permute-start.3 = (bf16[64,768]{1,0:T(8,128)(2,1)S(1)}, bf16[64,768]{1,0:T(8,128)(2,1)S(1)}, u32[]{:S(2)}, u32[]{:S(2)}) collective-permute-start(bf16[64,768]{1,0:T(8,128)(2,1)S(1)} %select_reduce_fusion), channel_id=1, source_target_pairs={{0,1},{1,2},{2,3},{3,0},{4,5},{5,6},{6,7},{7,4},{8,9},{9,10},{10,1... | collective-permute-start | bytes 294920 | tf_op jit(solution)/shard_map/ppermute | solution.py:142
  94.0 0.6 copy-start.8
  103.8 2.1 %copy-start.6 = (bf16[64,768]{1,0:T(8,128)(2,1)}, bf16[64,768]{1,0:T(8,128)(2,1)S(1)}, u32[]{:S(2)}) copy-start(bf16[64,768]{1,0:T(8,128)(2,1)S(1)} %multiply_convert_fusion.1) | copy-start | bytes 294916
  105.9 28.7 %all-to-all-start.2 = ((bf16[8,64,1024]{2,1,0:T(8,128)(2,1)}), bf16[8,64,1024]{2,1,0:T(8,128)(2,1)S(1)}, u32[]{:S(2)}, u32[]{:S(2)}) async-start(bf16[8,64,1024]{2,1,0:T(8,128)(2,1)} %bitcast.44), calls=%async_computation.3 | async-start | bytes 2097152 | tf_op jit(solution)/shard_map/all_to_all | solution.py:154
  134.6 29.7 %all-to-all-start.3 = ((bf16[8,64,1024]{2,1,0:T(8,128)(2,1)}), bf16[8,64,1024]{2,1,0:T(8,128)(2,1)}, u32[]{:S(2)}, u32[]{:S(2)}) async-start(bf16[8,64,1024]{2,1,0:T(8,128)(2,1)} %bitcast.43), calls=%async_computation.4 | async-start | bytes 2097152 | tf_op jit(solution)/shard_map/all_to_all | solution.py:162
  139.4 1.2 copy-start.1
  164.3 1.2 copy-start.2
  169.7 11.1 %copy-start.5 = (bf16[8,64,1024]{2,1,0:T(8,128)(2,1)S(1)}, bf16[8,64,1024]{2,1,0:T(8,128)(2,1)}, u32[]{:S(2)}) copy-start(bf16[8,64,1024]{2,1,0:T(8,128)(2,1)} %copy-done.4) | copy-start | bytes 3145732
  169.7 11.1 %copy-start.7 = (bf16[64,768]{1,0:T(8,128)(2,1)S(1)}, bf16[64,768]{1,0:T(8,128)(2,1)}, u32[]{:S(2)}) copy-start(bf16[64,768]{1,0:T(8,128)(2,1)} %copy-done.6) | copy-start | bytes 294916
Sparse Core Ops, SparseCore 0:
  9.6 49.0 all-gather.1
  61.2 62.5 reduce-scatter.1

commit v2 on v1

--- a/solution.py
+++ b/solution.py
@@ -22,25 +22,26 @@
     return jnp.sum(jnp.where(match, tenant_storage_row[None, None, :], 0), axis=2)
 
 
-def pick_kernel(which_ref, in_ref, out_ref):
-    out_ref[...] = in_ref[...]
+def pick_kernel(count, which_ref, in_ref, out_ref):
+    for j in range(count):
+        out_ref[j] = in_ref[which_ref[j]]
 
 
 def pick(which, table):
     count = which.shape[0]
     _, rank, width = table.shape
     return pl.pallas_call(
-        pick_kernel,
+        functools.partial(pick_kernel, count),
         out_shape=jax.ShapeDtypeStruct((count, rank, width), table.dtype),
-        grid_spec=pltpu.PrefetchScalarGridSpec(
-            num_scalar_prefetch=1,
-            grid=(count,),
-            in_specs=[pl.BlockSpec((1, rank, width), lambda j, which_ref: (which_ref[j], 0, 0))],
-            out_specs=pl.BlockSpec((1, rank, width), lambda j, which_ref: (j, 0, 0)),
-        ),
+        in_specs=[
+            pl.BlockSpec(memory_space=pltpu.SMEM),
+            pl.BlockSpec(memory_space=pltpu.VMEM),
+        ],
+        out_specs=pl.BlockSpec(memory_space=pltpu.VMEM),
         cost_estimate=pl.CostEstimate(
             flops=0, transcendentals=0, bytes_accessed=2 * count * rank * width * 2
         ),
+        compiler_params=pltpu.CompilerParams(vmem_limit_bytes=16 * 1024 * 1024),
         name="pick",
     )(which, table)
 
@@ -111,15 +112,18 @@
     up_out = pick(send_row, adapter_up)
     down_out = pick(send_row, adapter_down)
     up = lax.all_to_all(up_out, "seq", split_axis=0, concat_axis=0, tiled=True)
+    base_terms = jnp.dot(
+        attention_output, output_weight, preferred_element_type=jnp.float32
+    ).astype(jnp.bfloat16)
+    up, down_out, base_terms = lax.optimization_barrier((up, down_out, base_terms))
+    base_output = lax.psum_scatter(
+        base_terms, "tp", scatter_dimension=1, tiled=True
+    ).astype(jnp.float32)
     up = up.reshape(seq_count * rank, width)
     down = lax.all_to_all(down_out, "seq", split_axis=0, concat_axis=0, tiled=True)
     down = down.reshape(seq_count * rank, width)
 
     gathered = lax.all_gather(output_gradient, "tp", axis=1, tiled=True)
-    base_terms = jnp.dot(attention_output, output_weight, preferred_element_type=jnp.float32)
-    base_output = lax.psum_scatter(
-        base_terms.astype(jnp.bfloat16), "tp", scatter_dimension=1, tiled=True
-    ).astype(jnp.float32)
 
     my_owner = lax.dynamic_index_in_dim(owner, device, 0, keepdims=False)
     counts = lax.dynamic_index_in_dim(slot_token_rows, device, 0, keepdims=False)
@@ -151,6 +155,7 @@
     part_down = jnp.dot(
         spread_grad, attention_output, preferred_element_type=jnp.float32
     ).astype(jnp.bfloat16)
+    part_down, gathered, down = lax.optimization_barrier((part_down, gathered, down))
     incoming_down = lax.all_to_all(
         part_down.reshape(seq_count, rank, width), "seq", split_axis=0, concat_axis=0, tiled=True
     )
@@ -159,10 +164,6 @@
     part_up = (
         adapter_scale * jnp.dot(spread_low, output_gradient, preferred_element_type=jnp.float32)
     ).astype(jnp.bfloat16)
-    incoming_up = lax.all_to_all(
-        part_up.reshape(seq_count, rank, width), "seq", split_axis=0, concat_axis=0, tiled=True
-    )
-
     back_base = lax.dot_general(
         gathered, output_weight, contract_last, preferred_element_type=jnp.float32
     )
@@ -170,6 +171,11 @@
         back_base
         + lax.dot_general(spread_grad, down, contract_leading, preferred_element_type=jnp.float32)
     ).astype(jnp.bfloat16)
+    part_up, incoming_down, in_grad = lax.optimization_barrier((part_up, incoming_down, in_grad))
+    incoming_up = lax.all_to_all(
+        part_up.reshape(seq_count, rank, width), "seq", split_axis=0, concat_axis=0, tiled=True
+    )
+
     out_act = (
         base_output
         + adapter_scale

time: 195 us -> 154 us (0.79)
  waiting for transfers between devices: 92.3 us -> 63.1 us
  Pallas kernels: 17.9 us -> 10.6 us
    all_to_all x1, waiting for transfers between devices: 21.8 us -> 10.9 us  [local(): lax.all_to_all(part_down.reshape(seq_count, rank, width), 'seq', split_ax...]
    all_to_all x1, waiting for transfers between devices: 20.5 us -> 9.64 us  [local(): lax.all_to_all(down_out, 'seq', split_axis=0, concat_axis=0, tiled=True)]
    all_to_all x1, waiting for transfers between devices: 20.8 us -> 11.1 us  [local(): up = lax.all_to_all(up_out, 'seq', split_axis=0, concat_axis=0, tiled=True)]
    pallas_call x2, Pallas kernels: 10.5 us -> 3.16 us  [pick(): pl.pallas_call(functools.partial(pick_kernel, count), out_shape=jax.Shape...]
    all_to_all x1, starting transfers between devices: 7.31 us -> 3.59 us  [local(): lax.all_to_all(down_out, 'seq', split_axis=0, concat_axis=0, tiled=True)]
    all_to_all x1, starting transfers between devices: 4.24 us -> 7.28 us  [local(): up = lax.all_to_all(up_out, 'seq', split_axis=0, concat_axis=0, tiled=True)]
    unnamed x25 -> x23, local copies, waits for them, and re-layouts: 4.49 us -> 2.75 us
  transfers between devices with their start and end apart: 12 -> 12, of which waited for: 7 -> 6; matrix products, arithmetic and copies ran while one was open for 20% -> 24% of each run, Pallas kernels for 9% -> 7%
where the time goes in v2:
time: 154 us
  waiting for transfers between devices  63.1 us (41%)
  matrix products  38 us (25%)
  starting transfers between devices  22.5 us (15%)
  between operations  14.2 us (9%)
  Pallas kernels  10.6 us (7%)
  local copies, waits for them, and re-layouts  3.1 us (2%)
  other arithmetic  2.02 us (1%)
    all_to_all x1, waiting for transfers between devices, local(): lax.all_to_all(part_up.reshape(seq_count, rank, width), 'seq', split_axis...  21.5 us
    dot_general x1, matrix products, local(): jnp.dot(attention_output, output_weight, preferred_element_type=jnp.float32)  13.2 us
    all_to_all x1, waiting for transfers between devices, local(): up = lax.all_to_all(up_out, 'seq', split_axis=0, concat_axis=0, tiled=True)  11.1 us
    dot_general x1, matrix products, local(): lax.dot_general(gathered, output_weight, contract_last, preferred_element...  11.1 us
    all_to_all x1, waiting for transfers between devices, local(): lax.all_to_all(part_down.reshape(seq_count, rank, width), 'seq', split_ax...  10.9 us
    all_to_all x1, waiting for transfers between devices, local(): lax.all_to_all(down_out, 'seq', split_axis=0, concat_axis=0, tiled=True)  9.64 us
    ppermute x6, waiting for transfers between devices, project(): total = total + lax.ppermute(part, 'tp', order).astype(jnp.float32)  9.31 us
    pallas_call x2, Pallas kernels, lion(): pl.pallas_call(functools.partial(lion_kernel, seq_count, owned), out_shap...  7.45 us
  transfers between devices with their start and end apart: 12, of which 6 were waited for; matrix products, arithmetic and copies ran while one was open for 24% of the time, Pallas kernels for 7%

profile of v2, /device:TPU:0, one launch (start us, length us, event | category | flops | bytes accessed | tf_op | source)
XLA Modules:
  0.0 153.6 jit_solution(5758159670872866901)
XLA Ops:
  7.3 0.7 all-gather.2.cloned.1.call-update
  8.0 0.2 select_reduce_fusion.2
  8.4 1.6 %pick.2 = bf16[8,64,1024]{2,1,0:T(8,128)(2,1)} custom-call(s32[8]{0:T(128)S(1)} %get-tuple-element.34.which_ref, bf16[4,64,1024]{2,1,0:T(8,128)(2,1)S(1)} %copy-done.3), custom_call_target="tpu_custom_call" | custom-call | bytes 2097152 | tf_op jit(solution)/shard_map/pick/pallas_call | solution.py:33
  10.0 7.3 %all-to-all-start = ((bf16[8,64,1024]{2,1,0:T(8,128)(2,1)}), bf16[8,64,1024]{2,1,0:T(8,128)(2,1)}, u32[]{:S(2)}, u32[]{:S(2)}) async-start(bf16[8,64,1024]{2,1,0:T(8,128)(2,1)} %pick.2), calls=%async_computation | async-start | bytes 2097152 | tf_op jit(solution)/shard_map/all_to_all | solution.py:114
  17.3 1.6 %pick.3 = bf16[8,64,1024]{2,1,0:T(8,128)(2,1)} custom-call(s32[8]{0:T(128)S(1)} %get-tuple-element.34.which_ref, bf16[4,64,1024]{2,1,0:T(8,128)(2,1)S(1)} %copy-done.4), custom_call_target="tpu_custom_call" | custom-call | bytes 2097152 | tf_op jit(solution)/shard_map/pick/pallas_call | solution.py:33
  18.9 13.2 %convolution_convert_fusion = bf16[768,4096]{1,0:T(8,128)(2,1)} fusion(bf16[768,1024]{1,0:T(8,128)(2,1)S(1)} %copy-done, bf16[1024,4096]{1,0:T(8,128)(2,1)} %param.12), kind=kOutput, calls=%fused_computation | convolution fusion | flops 6445596672 | bytes 16252928 | tf_op jit(solution)/shard_map/dot_general | solution.py:115
  32.0 11.1 %all-to-all-done = bf16[8,64,1024]{2,1,0:T(8,128)(2,1)} async-done(((bf16[8,64,1024]{2,1,0:T(8,128)(2,1)}), bf16[8,64,1024]{2,1,0:T(8,128)(2,1)}, u32[]{:S(2)}, u32[]{:S(2)}) %all-to-all-start) | async-done | bytes 1048608 | tf_op jit(solution)/shard_map/all_to_all | solution.py:114
  43.1 0.2 dynamic-slice_reduce_fusion
  43.4 3.6 %all-to-all-start.1 = ((bf16[8,64,1024]{2,1,0:T(8,128)(2,1)}), bf16[8,64,1024]{2,1,0:T(8,128)(2,1)S(1)}, u32[]{:S(2)}, u32[]{:S(2)}) async-start(bf16[8,64,1024]{2,1,0:T(8,128)(2,1)} %pick.3), calls=%async_computation.2 | async-start | bytes 2097152 | tf_op jit(solution)/shard_map/all_to_all | solution.py:123
  47.3 2.8 %select_reduce_fusion.1 = bf16[64,768]{1,0:T(8,128)(2,1)S(1)} fusion(bf16[8,64,1024]{2,1,0:T(8,128)(2,1)} %all-to-all-done, bf16[768,1024]{1,0:T(8,128)(2,1)} %param.11, pred[8,768]{1,0:T(8,128)(4,1)S(1)} %fusion.6), kind=kOutput, calls=%fused_computation.9 | convolution fusion | flops 806043648 | bytes 2725888 | tf_op jit(solution)/shard_map/dot_general | solution.py:140
  50.1 0.9 collective-permute-start.2
  51.0 0.8 collective-permute-start.1
  51.8 0.2 collective-permute-start
  51.9 4.2 %collective-permute-done.2 = bf16[64,768]{1,0:T(8,128)(2,1)S(1)} collective-permute-done((bf16[64,768]{1,0:T(8,128)(2,1)S(1)}, bf16[64,768]{1,0:T(8,128)(2,1)S(1)}, u32[]{:S(2)}, u32[]{:S(2)}) %collective-permute-start.2) | collective-permute-done | bytes 98336 | tf_op jit(solution)/shard_map/ppermute | solution.py:146
  56.2 5.1 %collective-permute-done.1 = bf16[64,768]{1,0:T(8,128)(2,1)S(1)} collective-permute-done((bf16[64,768]{1,0:T(8,128)(2,1)S(1)}, bf16[64,768]{1,0:T(8,128)(2,1)S(1)}, u32[]{:S(2)}, u32[]{:S(2)}) %collective-permute-start.1) | collective-permute-done | bytes 98336 | tf_op jit(solution)/shard_map/ppermute | solution.py:146
  61.4 2.0 %convolution_convert_fusion.1 = bf16[512,1024]{1,0:T(8,128)(2,1)} fusion(bf16[512,768]{1,0:T(8,128)(2,1)S(1)} %bitcast.40, bf16[768,1024]{1,0:T(8,128)(2,1)S(1)} %copy-done), kind=kOutput, calls=%fused_computation.10 | convolution fusion | flops 805830656 | bytes 3407872 | tf_op jit(solution)/shard_map/dot_general | solution.py:155
  63.3 9.6 %all-to-all-done.1 = bf16[8,64,1024]{2,1,0:T(8,128)(2,1)S(1)} async-done(((bf16[8,64,1024]{2,1,0:T(8,128)(2,1)}), bf16[8,64,1024]{2,1,0:T(8,128)(2,1)S(1)}, u32[]{:S(2)}, u32[]{:S(2)}) %all-to-all-start.1) | async-done | bytes 1048608 | tf_op jit(solution)/shard_map/all_to_all | solution.py:123
  73.0 1.0 fusion.11
  74.2 1.6 %collective-permute-start.4 = (bf16[64,768]{1,0:T(8,128)(2,1)S(1)}, bf16[64,768]{1,0:T(8,128)(2,1)}, u32[]{:S(2)}, u32[]{:S(2)}) collective-permute-start(bf16[64,768]{1,0:T(8,128)(2,1)S(1)} %select_reduce_fusion), channel_id=1, source_target_pairs={{0,2},{1,3},{2,0},{3,1},{4,6},{5,7},{6,4},{7,5},{8,10},{9,11},{10,... | collective-permute-start | bytes 294920 | tf_op jit(solution)/shard_map/ppermute | solution.py:146
  75.9 3.6 %all-to-all-start.2 = ((bf16[8,64,1024]{2,1,0:T(8,128)(2,1)}), bf16[8,64,1024]{2,1,0:T(8,128)(2,1)S(1)}, u32[]{:S(2)}, u32[]{:S(2)}) async-start(bf16[8,64,1024]{2,1,0:T(8,128)(2,1)} %bitcast.43), calls=%async_computation.3 | async-start | bytes 2097152 | tf_op jit(solution)/shard_map/all_to_all | solution.py:159
  79.6 11.1 %fusion.12 = f32[768,1024]{1,0:T(8,128)S(1)} fusion(bf16[768,4096]{1,0:T(8,128)(2,1)} %all-gather.2.cloned.1.call-done, bf16[1024,4096]{1,0:T(8,128)(2,1)} %param.12), kind=kOutput, calls=%fused_computation.46 | convolution fusion | flops 6442450944 | bytes 17825792 | tf_op jit(solution)/shard_map/dot_general | solution.py:167
  90.6 2.2 %add_convert_fusion = bf16[768,1024]{1,0:T(8,128)(2,1)} fusion(f32[768,1024]{1,0:T(8,128)S(1)} %fusion.12, bf16[512,768]{1,0:T(8,128)(2,1)S(1)} %bitcast.41, bf16[512,1024]{1,0:T(8,128)(2,1)S(1)} %bitcast.39), kind=kOutput, calls=%fused_computation.4 | convolution fusion | flops 806879232 | bytes 6553600 | tf_op jit(solution)/shard_map/dot_general | solution.py:172
  92.8 1.0 add_convert_fusion.1
  93.9 2.0 %multiply_convert_fusion = bf16[512,1024]{1,0:T(8,128)(2,1)} fusion(bf16[512,768]{1,0:T(8,128)(2,1)S(1)} %bitcast.45, bf16[768,1024]{1,0:T(8,128)(2,1)S(1)} %copy-done.7), kind=kOutput, calls=%fused_computation.5 | convolution fusion | flops 806354944 | bytes 3407872 | tf_op jit(solution)/shard_map/dot_general | solution.py:165
  95.9 10.9 %all-to-all-done.2.incoming_ref = bf16[8,64,1024]{2,1,0:T(8,128)(2,1)S(1)} async-done(((bf16[8,64,1024]{2,1,0:T(8,128)(2,1)}), bf16[8,64,1024]{2,1,0:T(8,128)(2,1)S(1)}, u32[]{:S(2)}, u32[]{:S(2)}) %all-to-all-start.2) | async-done | bytes 1048608 | tf_op jit(solution)/shard_map/all_to_all | solution.py:159
  106.8 4.2 %all-to-all-start.3 = ((bf16[8,64,1024]{2,1,0:T(8,128)(2,1)}), bf16[8,64,1024]{2,1,0:T(8,128)(2,1)}, u32[]{:S(2)}, u32[]{:S(2)}) async-start(bf16[8,64,1024]{2,1,0:T(8,128)(2,1)} %bitcast.44), calls=%async_computation.4 | async-start | bytes 2097152 | tf_op jit(solution)/shard_map/all_to_all | solution.py:175
  111.4 1.2 copy-done.1
  112.6 3.3 %lion.2 = (f32[4,64,1024]{2,1,0:T(8,128)}, f32[4,64,1024]{2,1,0:T(8,128)}) custom-call(f32[32]{0:T(128)S(1)} %reshape.117.choose_ref, f32[4]{0:T(128)S(1)} %maximum_convert_fusion.scale_ref, bf16[8,64,1024]{2,1,0:T(8,128)(2,1)S(1)} %all-to-all-done.2.incoming_ref, f32[4,64,1024]{2,1,0:T(8,128)S(1)} %copy-done.1), custom_call_target="tpu_custom_call" | custom-call | flops 4194304 | bytes 4194304 | tf_op jit(solution)/shard_map/lion/pallas_call | solution.py:70
  115.9 21.5 %all-to-all-done.3.incoming_ref = bf16[8,64,1024]{2,1,0:T(8,128)(2,1)} async-done(((bf16[8,64,1024]{2,1,0:T(8,128)(2,1)}), bf16[8,64,1024]{2,1,0:T(8,128)(2,1)}, u32[]{:S(2)}, u32[]{:S(2)}) %all-to-all-start.3) | async-done | bytes 1048608 | tf_op jit(solution)/shard_map/all_to_all | solution.py:175
  137.4 1.2 copy-done.2
  138.6 4.2 %lion.3 = (f32[4,64,1024]{2,1,0:T(8,128)}, f32[4,64,1024]{2,1,0:T(8,128)}) custom-call(f32[32]{0:T(128)S(1)} %reshape.117.choose_ref, f32[4]{0:T(128)S(1)} %maximum_convert_fusion.scale_ref, bf16[8,64,1024]{2,1,0:T(8,128)(2,1)} %all-to-all-done.3.incoming_ref, f32[4,64,1024]{2,1,0:T(8,128)S(1)} %copy-done.2), custom_call_target="tpu_custom_call" | custom-call | flops 4194304 | bytes 4194304 | tf_op jit(solution)/shard_map/lion/pallas_call | solution.py:70
  142.8 3.9 %fusion.1 = bf16[768,1024]{1,0:T(8,128)(2,1)} fusion(bf16[768,1024]{1,0:T(8,128)(2,1)} %reduce-scatter.2.cloned.1.call-done, bf16[8,64,1024]{2,1,0:T(8,128)(2,1)} %all-to-all-done, pred[8,768]{1,0:T(8,128)(4,1)S(1)} %fusion.6, bf16[64,768]{1,0:T(8,128)(2,1)S(1)} %add_convert_fusion.1), kind=kOutput, calls=%fused_computation.3 | convolution fusion | flops 808845312 | bytes 4298752 | tf_op jit(solution)/shard_map/dot_general | solution.py:182
  (46 shorter events, 1.6 us)
Async XLA Ops:
  7.2 11.7 %copy-start = (bf16[768,1024]{1,0:T(8,128)(2,1)S(1)}, bf16[768,1024]{1,0:T(8,128)(2,1)}, u32[]{:S(2)}) copy-start(bf16[768,1024]{1,0:T(8,128)(2,1)} %param.10) | copy-start | bytes 4718596
  7.2 0.8 copy-start.10
  7.2 0.8 copy-start.9
  7.2 1.2 copy-start.3
  7.2 65.8 %all-gather.2.cloned.1.call-start = ((), (), s32[]{:S(2)}) async-start(), calls=%async_computation.6 | async-start | bytes 7864320 | tf_op jit(solution)/shard_map/all_gather | solution.py:126
  8.4 8.9 %copy-start.4 = (bf16[4,64,1024]{2,1,0:T(8,128)(2,1)S(1)}, bf16[4,64,1024]{2,1,0:T(8,128)(2,1)}, u32[]{:S(2)}) copy-start(bf16[4,64,1024]{2,1,0:T(8,128)(2,1)} %in_ref.3) | copy-start | bytes 1572868
  10.0 33.2 %all-to-all-start = ((bf16[8,64,1024]{2,1,0:T(8,128)(2,1)}), bf16[8,64,1024]{2,1,0:T(8,128)(2,1)}, u32[]{:S(2)}, u32[]{:S(2)}) async-start(bf16[8,64,1024]{2,1,0:T(8,128)(2,1)} %pick.2), calls=%async_computation | async-start | bytes 2097152 | tf_op jit(solution)/shard_map/all_to_all | solution.py:114
  17.2 125.6 %reduce-scatter.2.cloned.1.call-start = ((), (), s32[]{:S(2)}) async-start(), calls=%async_computation.5 | async-start | bytes 7864320 | tf_op jit(solution)/shard_map/reduce_scatter | solution.py:119
  32.0 11.1 %copy-start.8 = (s32[8,4]{0,1:T(4,128)S(1)}, s32[8,4]{0,1:T(4,128)}, u32[]{:S(2)}) copy-start(s32[8,4]{0,1:T(4,128)} %param.19) | copy-start | bytes 388
  43.4 29.5 %all-to-all-start.1 = ((bf16[8,64,1024]{2,1,0:T(8,128)(2,1)}), bf16[8,64,1024]{2,1,0:T(8,128)(2,1)S(1)}, u32[]{:S(2)}, u32[]{:S(2)}) async-start(bf16[8,64,1024]{2,1,0:T(8,128)(2,1)} %pick.3), calls=%async_computation.2 | async-start | bytes 2097152 | tf_op jit(solution)/shard_map/all_to_all | solution.py:123
  50.1 6.1 %collective-permute-start.2 = (bf16[64,768]{1,0:T(8,128)(2,1)S(1)}, bf16[64,768]{1,0:T(8,128)(2,1)S(1)}, u32[]{:S(2)}, u32[]{:S(2)}) collective-permute-start(bf16[64,768]{1,0:T(8,128)(2,1)S(1)} %select_reduce_fusion.1), channel_id=1, source_target_pairs={{0,3},{1,0},{2,1},{3,2},{4,7},{5,4},{6,5},{7,6},{8,11},{9,8},{10,9... | collective-permute-start | bytes 294920 | tf_op jit(solution)/shard_map/ppermute | solution.py:146
  51.0 10.3 %collective-permute-start.1 = (bf16[64,768]{1,0:T(8,128)(2,1)S(1)}, bf16[64,768]{1,0:T(8,128)(2,1)S(1)}, u32[]{:S(2)}, u32[]{:S(2)}) collective-permute-start(bf16[64,768]{1,0:T(8,128)(2,1)S(1)} %select_reduce_fusion.1), channel_id=1, source_target_pairs={{0,2},{1,3},{2,0},{3,1},{4,6},{5,7},{6,4},{7,5},{8,10},{9,11},{10,... | collective-permute-start | bytes 294920 | tf_op jit(solution)/shard_map/ppermute | solution.py:146
  51.8 9.5 %collective-permute-start = (bf16[64,768]{1,0:T(8,128)(2,1)S(1)}, bf16[64,768]{1,0:T(8,128)(2,1)S(1)}, u32[]{:S(2)}, u32[]{:S(2)}) collective-permute-start(bf16[64,768]{1,0:T(8,128)(2,1)S(1)} %select_reduce_fusion.1), channel_id=1, source_target_pairs={{0,1},{1,2},{2,3},{3,0},{4,5},{5,6},{6,7},{7,4},{8,9},{9,10},{10,1... | collective-permute-start | bytes 294920 | tf_op jit(solution)/shard_map/ppermute | solution.py:146
  73.0 1.0 copy-start.5
  74.1 18.7 %collective-permute-start.5 = (bf16[64,768]{1,0:T(8,128)(2,1)S(1)}, bf16[64,768]{1,0:T(8,128)(2,1)}, u32[]{:S(2)}, u32[]{:S(2)}) collective-permute-start(bf16[64,768]{1,0:T(8,128)(2,1)S(1)} %select_reduce_fusion), channel_id=1, source_target_pairs={{0,3},{1,0},{2,1},{3,2},{4,7},{5,4},{6,5},{7,6},{8,11},{9,8},{10,9... | collective-permute-start | bytes 294920 | tf_op jit(solution)/shard_map/ppermute | solution.py:146
  74.2 18.6 %collective-permute-start.4 = (bf16[64,768]{1,0:T(8,128)(2,1)S(1)}, bf16[64,768]{1,0:T(8,128)(2,1)}, u32[]{:S(2)}, u32[]{:S(2)}) collective-permute-start(bf16[64,768]{1,0:T(8,128)(2,1)S(1)} %select_reduce_fusion), channel_id=1, source_target_pairs={{0,2},{1,3},{2,0},{3,1},{4,6},{5,7},{6,4},{7,5},{8,10},{9,11},{10,... | collective-permute-start | bytes 294920 | tf_op jit(solution)/shard_map/ppermute | solution.py:146
  75.8 17.0 %collective-permute-start.3 = (bf16[64,768]{1,0:T(8,128)(2,1)S(1)}, bf16[64,768]{1,0:T(8,128)(2,1)}, u32[]{:S(2)}, u32[]{:S(2)}) collective-permute-start(bf16[64,768]{1,0:T(8,128)(2,1)S(1)} %select_reduce_fusion), channel_id=1, source_target_pairs={{0,1},{1,2},{2,3},{3,0},{4,5},{5,6},{6,7},{7,4},{8,9},{9,10},{10,1... | collective-permute-start | bytes 294920 | tf_op jit(solution)/shard_map/ppermute | solution.py:146
  75.9 30.9 %all-to-all-start.2 = ((bf16[8,64,1024]{2,1,0:T(8,128)(2,1)}), bf16[8,64,1024]{2,1,0:T(8,128)(2,1)S(1)}, u32[]{:S(2)}, u32[]{:S(2)}) async-start(bf16[8,64,1024]{2,1,0:T(8,128)(2,1)} %bitcast.43), calls=%async_computation.3 | async-start | bytes 2097152 | tf_op jit(solution)/shard_map/all_to_all | solution.py:159
  79.6 11.1 %copy-start.6 = (bf16[8,64,1024]{2,1,0:T(8,128)(2,1)S(1)}, bf16[8,64,1024]{2,1,0:T(8,128)(2,1)}, u32[]{:S(2)}) copy-start(bf16[8,64,1024]{2,1,0:T(8,128)(2,1)} %copy-done.5) | copy-start | bytes 3145732
  90.6 3.3 %copy-start.7 = (bf16[768,1024]{1,0:T(8,128)(2,1)S(1)}, bf16[768,1024]{1,0:T(8,128)(2,1)}, u32[]{:S(2)}) copy-start(bf16[768,1024]{1,0:T(8,128)(2,1)} %param.11) | copy-start | bytes 4718596
  106.8 30.6 %all-to-all-start.3 = ((bf16[8,64,1024]{2,1,0:T(8,128)(2,1)}), bf16[8,64,1024]{2,1,0:T(8,128)(2,1)}, u32[]{:S(2)}, u32[]{:S(2)}) async-start(bf16[8,64,1024]{2,1,0:T(8,128)(2,1)} %bitcast.44), calls=%async_computation.4 | async-start | bytes 2097152 | tf_op jit(solution)/shard_map/all_to_all | solution.py:175
  111.4 1.2 copy-start.1
  137.4 1.2 copy-start.2
Sparse Core Ops, SparseCore 0:
  9.6 53.0 all-gather.1
  65.3 57.8 reduce-scatter.1

commit v3 on v2

--- a/solution.py
+++ b/solution.py
@@ -46,13 +46,13 @@
     )(which, table)
 
 
-def lion_kernel(seq_count, owned, choose_ref, scale_ref, incoming_ref, moment_ref, step_ref, new_ref):
+def lion_kernel(seq_count, owned, row_ref, used_ref, scale_ref, incoming_ref, moment_ref, step_ref, new_ref, total):
+    total[...] = jnp.zeros_like(total)
+    for i in range(seq_count):
+        k = row_ref[i]
+        total[k] = total[k] + used_ref[i] * incoming_ref[i].astype(jnp.float32)
     for k in range(owned):
-        total = None
-        for i in range(seq_count):
-            term = choose_ref[i * owned + k] * incoming_ref[i].astype(jnp.float32)
-            total = term if total is None else total + term
-        grad = total / scale_ref[k]
+        grad = total[k] / scale_ref[k]
         moment = moment_ref[k]
         combined = beta_first * moment + (1.0 - beta_first) * grad
         spread = jnp.sqrt(jnp.mean(combined * combined, axis=0, keepdims=True) + epsilon)
@@ -60,7 +60,7 @@
         new_ref[k] = beta_second * moment + (1.0 - beta_second) * grad
 
 
-def lion(choose, denom, incoming, moment):
+def lion(row, used, denom, incoming, moment):
     seq_count, rank, width = incoming.shape
     owned = moment.shape[0]
     tile = min(256, width)
@@ -71,16 +71,18 @@
         functools.partial(lion_kernel, seq_count, owned),
         out_shape=(shape, shape),
         grid=(width // tile,),
-        in_specs=[smem, smem, pl.BlockSpec((seq_count, rank, tile), lambda j: (0, 0, j)), block],
+        in_specs=[smem] * 3
+        + [pl.BlockSpec((seq_count, rank, tile), lambda j: (0, 0, j)), block],
         out_specs=(block, block),
+        scratch_shapes=[pltpu.VMEM((owned, rank, tile), jnp.float32)],
         cost_estimate=pl.CostEstimate(
-            flops=2 * owned * seq_count * rank * width,
+            flops=2 * seq_count * rank * width,
             transcendentals=owned * rank * width,
             bytes_accessed=seq_count * rank * width * 2 + 3 * owned * rank * width * 4,
         ),
-        compiler_params=pltpu.CompilerParams(vmem_limit_bytes=32 * 1024 * 1024),
+        compiler_params=pltpu.CompilerParams(vmem_limit_bytes=24 * 1024 * 1024),
         name="lion",
-    )(choose, denom, incoming, moment)
+    )(row, used, denom, incoming, moment)
 
 
 def local(
@@ -183,11 +185,12 @@
     ).astype(jnp.bfloat16)
 
     here = mine[:, :, None] & (within[:, :, None] == owned_ids[None, None, :])
-    choose = jnp.sum(here.astype(jnp.float32), axis=1).reshape(seq_count * owned)
+    used = jnp.sum(mine.astype(jnp.float32), axis=1)
     tokens_here = jnp.sum(jnp.where(here, slot_token_rows[:, :, None], 0), axis=(0, 1))
     denom = jnp.maximum(tokens_here, 1).astype(jnp.float32)
-    step_down, new_moment_down = lion(choose, denom, incoming_down, momentum_down)
-    step_up, new_moment_up = lion(choose, denom, incoming_up, momentum_up)
+    step_down, new_moment_down = lion(send_row, used, denom, incoming_down, momentum_down)
+    incoming_up, out_act = lax.optimization_barrier((incoming_up, out_act))
+    step_up, new_moment_up = lion(send_row, used, denom, incoming_up, momentum_up)
     return (out_act, in_grad, step_down, step_up, new_moment_down, new_moment_up)
 
 

time: 154 us -> 147 us (0.955)
  waiting for transfers between devices: 63.1 us -> 55.2 us
  starting transfers between devices: 22.5 us -> 25.5 us
    all_to_all x1, waiting for transfers between devices: 21.5 us -> 8.47 us  [local(): lax.all_to_all(part_up.reshape(seq_count, rank, width), 'seq', split_axis...]
    reduce_scatter x1, waiting for transfers between devices: 0.01 us -> 8.68 us  [local(): lax.psum_scatter(base_terms, 'tp', scatter_dimension=1, tiled=True)]
    ppermute x6, starting transfers between devices: 3.63 us -> 6.67 us  [project(): total = total + lax.ppermute(part, 'tp', order).astype(jnp.float32)]
    ppermute x6, waiting for transfers between devices: 9.31 us -> 7.02 us  [project(): total = total + lax.ppermute(part, 'tp', order).astype(jnp.float32)]
    all_to_all x1, waiting for transfers between devices: 10.9 us -> 8.82 us  [local(): lax.all_to_all(part_down.reshape(seq_count, rank, width), 'seq', split_ax...]
  transfers between devices with their start and end apart: 12 -> 12, of which waited for: 6 -> 7; matrix products, arithmetic and copies ran while one was open for 24% -> 27% of each run, Pallas kernels for 7% -> 4%
where the time goes in v3:
time: 147 us
  waiting for transfers between devices  55.2 us (38%)
  matrix products  38 us (26%)
  starting transfers between devices  25.5 us (17%)
  between operations  14.2 us (10%)
  Pallas kernels  10.1 us (7%)
  other arithmetic  2.03 us (1%)
  local copies, waits for them, and re-layouts  1.69 us (1%)
    dot_general x1, matrix products, local(): jnp.dot(attention_output, output_weight, preferred_element_type=jnp.float32)  13.2 us
    all_to_all x1, waiting for transfers between devices, local(): up = lax.all_to_all(up_out, 'seq', split_axis=0, concat_axis=0, tiled=True)  11.1 us
    dot_general x1, matrix products, local(): lax.dot_general(gathered, output_weight, contract_last, preferred_element...  11.1 us
    all_to_all x1, waiting for transfers between devices, local(): lax.all_to_all(down_out, 'seq', split_axis=0, concat_axis=0, tiled=True)  10.4 us
    all_to_all x1, waiting for transfers between devices, local(): lax.all_to_all(part_down.reshape(seq_count, rank, width), 'seq', split_ax...  8.82 us
    reduce_scatter x1, waiting for transfers between devices, local(): lax.psum_scatter(base_terms, 'tp', scatter_dimension=1, tiled=True)  8.68 us
    all_to_all x1, waiting for transfers between devices, local(): lax.all_to_all(part_up.reshape(seq_count, rank, width), 'seq', split_axis...  8.47 us
    all_to_all x1, starting transfers between devices, local(): up = lax.all_to_all(up_out, 'seq', split_axis=0, concat_axis=0, tiled=True)  7.28 us
  transfers between devices with their start and end apart: 12, of which 7 were waited for; matrix products, arithmetic and copies ran while one was open for 27% of the time, Pallas kernels for 4%

profile of v3, /device:TPU:0, one launch (start us, length us, event | category | flops | bytes accessed | tf_op | source)
XLA Modules:
  0.0 146.7 jit_solution(18345159733401588378)
XLA Ops:
  7.3 0.7 all-gather.2.cloned.1.call-update
  8.0 0.2 select_reduce_fusion.2
  8.4 1.6 %pick.2 = bf16[8,64,1024]{2,1,0:T(8,128)(2,1)} custom-call(s32[8]{0:T(128)S(1)} %get-tuple-element.41.which_ref.row_ref, bf16[4,64,1024]{2,1,0:T(8,128)(2,1)S(1)} %copy-done.3), custom_call_target="tpu_custom_call" | custom-call | bytes 2097152 | tf_op jit(solution)/shard_map/pick/pallas_call | solution.py:33
  10.0 7.3 %all-to-all-start = ((bf16[8,64,1024]{2,1,0:T(8,128)(2,1)}), bf16[8,64,1024]{2,1,0:T(8,128)(2,1)}, u32[]{:S(2)}, u32[]{:S(2)}) async-start(bf16[8,64,1024]{2,1,0:T(8,128)(2,1)} %pick.2), calls=%async_computation | async-start | bytes 2097152 | tf_op jit(solution)/shard_map/all_to_all | solution.py:116
  17.3 1.6 %pick.3 = bf16[8,64,1024]{2,1,0:T(8,128)(2,1)} custom-call(s32[8]{0:T(128)S(1)} %get-tuple-element.41.which_ref.row_ref, bf16[4,64,1024]{2,1,0:T(8,128)(2,1)S(1)} %copy-done.4), custom_call_target="tpu_custom_call" | custom-call | bytes 2097152 | tf_op jit(solution)/shard_map/pick/pallas_call | solution.py:33
  18.9 13.2 %convolution_convert_fusion = bf16[768,4096]{1,0:T(8,128)(2,1)} fusion(bf16[768,1024]{1,0:T(8,128)(2,1)S(1)} %copy-done, bf16[1024,4096]{1,0:T(8,128)(2,1)} %param.12), kind=kOutput, calls=%fused_computation | convolution fusion | flops 6445596672 | bytes 16252928 | tf_op jit(solution)/shard_map/dot_general | solution.py:117
  32.0 11.1 %all-to-all-done = bf16[8,64,1024]{2,1,0:T(8,128)(2,1)} async-done(((bf16[8,64,1024]{2,1,0:T(8,128)(2,1)}), bf16[8,64,1024]{2,1,0:T(8,128)(2,1)}, u32[]{:S(2)}, u32[]{:S(2)}) %all-to-all-start) | async-done | bytes 1048608 | tf_op jit(solution)/shard_map/all_to_all | solution.py:116
  43.1 0.2 dynamic-slice_reduce_fusion
  43.4 3.6 %all-to-all-start.1 = ((bf16[8,64,1024]{2,1,0:T(8,128)(2,1)}), bf16[8,64,1024]{2,1,0:T(8,128)(2,1)S(1)}, u32[]{:S(2)}, u32[]{:S(2)}) async-start(bf16[8,64,1024]{2,1,0:T(8,128)(2,1)} %pick.3), calls=%async_computation.1 | async-start | bytes 2097152 | tf_op jit(solution)/shard_map/all_to_all | solution.py:125
  47.3 2.8 %select_reduce_fusion.1 = bf16[64,768]{1,0:T(8,128)(2,1)S(1)} fusion(bf16[8,64,1024]{2,1,0:T(8,128)(2,1)} %all-to-all-done, bf16[768,1024]{1,0:T(8,128)(2,1)} %param.11, pred[8,768]{1,0:T(8,128)(4,1)S(1)} %fusion.6), kind=kOutput, calls=%fused_computation.9 | convolution fusion | flops 806043648 | bytes 2725888 | tf_op jit(solution)/shard_map/dot_general | solution.py:142
  50.1 1.6 %collective-permute-start.1 = (bf16[64,768]{1,0:T(8,128)(2,1)S(1)}, bf16[64,768]{1,0:T(8,128)(2,1)S(1)}, u32[]{:S(2)}, u32[]{:S(2)}) collective-permute-start(bf16[64,768]{1,0:T(8,128)(2,1)S(1)} %select_reduce_fusion.1), channel_id=1, source_target_pairs={{0,2},{1,3},{2,0},{3,1},{4,6},{5,7},{6,4},{7,5},{8,10},{9,11},{10,... | collective-permute-start | bytes 294920 | tf_op jit(solution)/shard_map/ppermute | solution.py:148
  51.7 1.7 %collective-permute-start.2 = (bf16[64,768]{1,0:T(8,128)(2,1)S(1)}, bf16[64,768]{1,0:T(8,128)(2,1)S(1)}, u32[]{:S(2)}, u32[]{:S(2)}) collective-permute-start(bf16[64,768]{1,0:T(8,128)(2,1)S(1)} %select_reduce_fusion.1), channel_id=1, source_target_pairs={{0,3},{1,0},{2,1},{3,2},{4,7},{5,4},{6,5},{7,6},{8,11},{9,8},{10,9... | collective-permute-start | bytes 294920 | tf_op jit(solution)/shard_map/ppermute | solution.py:148
  53.5 4.4 %collective-permute-done.1 = bf16[64,768]{1,0:T(8,128)(2,1)S(1)} collective-permute-done((bf16[64,768]{1,0:T(8,128)(2,1)S(1)}, bf16[64,768]{1,0:T(8,128)(2,1)S(1)}, u32[]{:S(2)}, u32[]{:S(2)}) %collective-permute-start.1) | collective-permute-done | bytes 98336 | tf_op jit(solution)/shard_map/ppermute | solution.py:148
  57.9 2.6 %collective-permute-done = bf16[64,768]{1,0:T(8,128)(2,1)S(1)} collective-permute-done((bf16[64,768]{1,0:T(8,128)(2,1)S(1)}, bf16[64,768]{1,0:T(8,128)(2,1)S(1)}, u32[]{:S(2)}, u32[]{:S(2)}) %collective-permute-start) | collective-permute-done | bytes 98336 | tf_op jit(solution)/shard_map/ppermute | solution.py:148
  60.6 2.0 %convolution_convert_fusion.1 = bf16[512,1024]{1,0:T(8,128)(2,1)} fusion(bf16[512,768]{1,0:T(8,128)(2,1)S(1)} %bitcast.40, bf16[768,1024]{1,0:T(8,128)(2,1)S(1)} %copy-done), kind=kOutput, calls=%fused_computation.10 | convolution fusion | flops 805830656 | bytes 3407872 | tf_op jit(solution)/shard_map/dot_general | solution.py:157
  62.6 10.4 %all-to-all-done.1 = bf16[8,64,1024]{2,1,0:T(8,128)(2,1)S(1)} async-done(((bf16[8,64,1024]{2,1,0:T(8,128)(2,1)}), bf16[8,64,1024]{2,1,0:T(8,128)(2,1)S(1)}, u32[]{:S(2)}, u32[]{:S(2)}) %all-to-all-start.1) | async-done | bytes 1048608 | tf_op jit(solution)/shard_map/all_to_all | solution.py:125
  73.0 1.0 fusion.11
  74.1 1.6 %collective-permute-start.4 = (bf16[64,768]{1,0:T(8,128)(2,1)S(1)}, bf16[64,768]{1,0:T(8,128)(2,1)}, u32[]{:S(2)}, u32[]{:S(2)}) collective-permute-start(bf16[64,768]{1,0:T(8,128)(2,1)S(1)} %select_reduce_fusion), channel_id=1, source_target_pairs={{0,2},{1,3},{2,0},{3,1},{4,6},{5,7},{6,4},{7,5},{8,10},{9,11},{10,... | collective-permute-start | bytes 294920 | tf_op jit(solution)/shard_map/ppermute | solution.py:148
  75.7 1.7 %collective-permute-start.5 = (bf16[64,768]{1,0:T(8,128)(2,1)S(1)}, bf16[64,768]{1,0:T(8,128)(2,1)}, u32[]{:S(2)}, u32[]{:S(2)}) collective-permute-start(bf16[64,768]{1,0:T(8,128)(2,1)S(1)} %select_reduce_fusion), channel_id=1, source_target_pairs={{0,3},{1,0},{2,1},{3,2},{4,7},{5,4},{6,5},{7,6},{8,11},{9,8},{10,9... | collective-permute-start | bytes 294920 | tf_op jit(solution)/shard_map/ppermute | solution.py:148
  77.5 3.6 %all-to-all-start.2 = ((bf16[8,64,1024]{2,1,0:T(8,128)(2,1)}), bf16[8,64,1024]{2,1,0:T(8,128)(2,1)S(1)}, u32[]{:S(2)}, u32[]{:S(2)}) async-start(bf16[8,64,1024]{2,1,0:T(8,128)(2,1)} %bitcast.43), calls=%async_computation.2 | async-start | bytes 2097152 | tf_op jit(solution)/shard_map/all_to_all | solution.py:161
  81.1 11.1 %fusion.12 = f32[768,1024]{1,0:T(8,128)S(1)} fusion(bf16[768,4096]{1,0:T(8,128)(2,1)} %all-gather.2.cloned.1.call-done, bf16[1024,4096]{1,0:T(8,128)(2,1)} %param.12), kind=kOutput, calls=%fused_computation.46 | convolution fusion | flops 6442450944 | bytes 17825792 | tf_op jit(solution)/shard_map/dot_general | solution.py:169
  92.2 2.2 %add_convert_fusion = bf16[768,1024]{1,0:T(8,128)(2,1)} fusion(f32[768,1024]{1,0:T(8,128)S(1)} %fusion.12, bf16[512,768]{1,0:T(8,128)(2,1)S(1)} %bitcast.41, bf16[512,1024]{1,0:T(8,128)(2,1)S(1)} %bitcast.39), kind=kOutput, calls=%fused_computation.4 | convolution fusion | flops 806879232 | bytes 6553600 | tf_op jit(solution)/shard_map/dot_general | solution.py:174
  94.3 1.0 add_convert_fusion.1
  95.5 2.0 %multiply_convert_fusion = bf16[512,1024]{1,0:T(8,128)(2,1)} fusion(bf16[512,768]{1,0:T(8,128)(2,1)S(1)} %bitcast.45, bf16[768,1024]{1,0:T(8,128)(2,1)S(1)} %copy-done.7), kind=kOutput, calls=%fused_computation.5 | convolution fusion | flops 806354944 | bytes 3407872 | tf_op jit(solution)/shard_map/dot_general | solution.py:167
  97.5 8.8 %all-to-all-done.2.incoming_ref = bf16[8,64,1024]{2,1,0:T(8,128)(2,1)S(1)} async-done(((bf16[8,64,1024]{2,1,0:T(8,128)(2,1)}), bf16[8,64,1024]{2,1,0:T(8,128)(2,1)S(1)}, u32[]{:S(2)}, u32[]{:S(2)}) %all-to-all-start.2) | async-done | bytes 1048608 | tf_op jit(solution)/shard_map/all_to_all | solution.py:161
  106.3 4.2 %all-to-all-start.3 = ((bf16[8,64,1024]{2,1,0:T(8,128)(2,1)}), bf16[8,64,1024]{2,1,0:T(8,128)(2,1)}, u32[]{:S(2)}, u32[]{:S(2)}) async-start(bf16[8,64,1024]{2,1,0:T(8,128)(2,1)} %bitcast.44), calls=%async_computation.3 | async-start | bytes 2097152 | tf_op jit(solution)/shard_map/all_to_all | solution.py:177
  110.7 1.2 copy-done.1
  111.9 3.0 %lion.2 = (f32[4,64,1024]{2,1,0:T(8,128)}, f32[4,64,1024]{2,1,0:T(8,128)}) custom-call(s32[8]{0:T(128)S(1)} %get-tuple-element.41.which_ref.row_ref, f32[8]{0:T(128)S(1)} %get-tuple-element.38.used_ref, f32[4]{0:T(128)S(1)} %maximum_convert_fusion.scale_ref, bf16[8,64,1024]{2,1,0:T(8,128)(2,1)S(1)} %all-to-all-done.2.incoming_ref, f32[4,64,1024]{2,1,0:T(8,128)S(1)} %copy-done.1), custom_call_target="tpu_custom_call" | custom-call | flops 1048576 | bytes 4194304 | tf_op jit(solution)/shard_map/lion/pallas_call | solution.py:70
  114.9 8.7 %reduce-scatter.2.cloned.1.call-done = bf16[768,1024]{1,0:T(8,128)(2,1)} async-done(((bf16[768,4096]{1,0:T(8,128)(2,1)}), bf16[768,1024]{1,0:T(8,128)(2,1)}) %reduce-scatter.2.cloned.1.call-update) | async-done | bytes 1572880 | tf_op jit(solution)/shard_map/reduce_scatter | solution.py:121
  123.5 3.9 %fusion.1 = bf16[768,1024]{1,0:T(8,128)(2,1)} fusion(bf16[768,1024]{1,0:T(8,128)(2,1)} %reduce-scatter.2.cloned.1.call-done, bf16[8,64,1024]{2,1,0:T(8,128)(2,1)} %all-to-all-done, pred[8,768]{1,0:T(8,128)(4,1)S(1)} %fusion.6, bf16[64,768]{1,0:T(8,128)(2,1)S(1)} %add_convert_fusion.1), kind=kOutput, calls=%fused_computation.3 | convolution fusion | flops 808845312 | bytes 4298752 | tf_op jit(solution)/shard_map/dot_general | solution.py:184
  127.5 8.5 %all-to-all-done.3.incoming_ref = bf16[8,64,1024]{2,1,0:T(8,128)(2,1)} async-done(((bf16[8,64,1024]{2,1,0:T(8,128)(2,1)}), bf16[8,64,1024]{2,1,0:T(8,128)(2,1)}, u32[]{:S(2)}, u32[]{:S(2)}) %all-to-all-start.3) | async-done | bytes 1048608 | tf_op jit(solution)/shard_map/all_to_all | solution.py:177
  135.9 4.0 %lion.3 = (f32[4,64,1024]{2,1,0:T(8,128)}, f32[4,64,1024]{2,1,0:T(8,128)}) custom-call(s32[8]{0:T(128)S(1)} %get-tuple-element.41.which_ref.row_ref, f32[8]{0:T(128)S(1)} %get-tuple-element.38.used_ref, f32[4]{0:T(128)S(1)} %maximum_convert_fusion.scale_ref, bf16[8,64,1024]{2,1,0:T(8,128)(2,1)} %all-to-all-done.3.incoming_ref, f32[4,64,1024]{2,1,0:T(8,128)S(1)} %copy-done.2), custom_call_target="tpu_custom_call" | custom-call | flops 1048576 | bytes 4194304 | tf_op jit(solution)/shard_map/lion/pallas_call | solution.py:70
  (44 shorter events, 1.2 us)
Async XLA Ops:
  7.2 11.7 %copy-start = (bf16[768,1024]{1,0:T(8,128)(2,1)S(1)}, bf16[768,1024]{1,0:T(8,128)(2,1)}, u32[]{:S(2)}) copy-start(bf16[768,1024]{1,0:T(8,128)(2,1)} %param.10) | copy-start | bytes 4718596
  7.2 0.8 copy-start.9
  7.2 0.8 copy-start.10
  7.2 1.2 copy-start.3
  7.2 65.8 %all-gather.2.cloned.1.call-start = ((), (), s32[]{:S(2)}) async-start(), calls=%async_computation.5 | async-start | bytes 7864320 | tf_op jit(solution)/shard_map/all_gather | solution.py:128
  8.4 8.9 %copy-start.4 = (bf16[4,64,1024]{2,1,0:T(8,128)(2,1)S(1)}, bf16[4,64,1024]{2,1,0:T(8,128)(2,1)}, u32[]{:S(2)}) copy-start(bf16[4,64,1024]{2,1,0:T(8,128)(2,1)} %in_ref.3) | copy-start | bytes 1572868
  10.0 33.2 %all-to-all-start = ((bf16[8,64,1024]{2,1,0:T(8,128)(2,1)}), bf16[8,64,1024]{2,1,0:T(8,128)(2,1)}, u32[]{:S(2)}, u32[]{:S(2)}) async-start(bf16[8,64,1024]{2,1,0:T(8,128)(2,1)} %pick.2), calls=%async_computation | async-start | bytes 2097152 | tf_op jit(solution)/shard_map/all_to_all | solution.py:116
  17.2 106.3 %reduce-scatter.2.cloned.1.call-start = ((), (), s32[]{:S(2)}) async-start(), calls=%async_computation.6 | async-start | bytes 7864320 | tf_op jit(solution)/shard_map/reduce_scatter | solution.py:121
  32.0 11.1 %copy-start.8 = (s32[8,4]{0,1:T(4,128)S(1)}, s32[8,4]{0,1:T(4,128)}, u32[]{:S(2)}) copy-start(s32[8,4]{0,1:T(4,128)} %param.19) | copy-start | bytes 388
  43.4 29.5 %all-to-all-start.1 = ((bf16[8,64,1024]{2,1,0:T(8,128)(2,1)}), bf16[8,64,1024]{2,1,0:T(8,128)(2,1)S(1)}, u32[]{:S(2)}, u32[]{:S(2)}) async-start(bf16[8,64,1024]{2,1,0:T(8,128)(2,1)} %pick.3), calls=%async_computation.1 | async-start | bytes 2097152 | tf_op jit(solution)/shard_map/all_to_all | solution.py:125
  50.1 7.8 %collective-permute-start.1 = (bf16[64,768]{1,0:T(8,128)(2,1)S(1)}, bf16[64,768]{1,0:T(8,128)(2,1)S(1)}, u32[]{:S(2)}, u32[]{:S(2)}) collective-permute-start(bf16[64,768]{1,0:T(8,128)(2,1)S(1)} %select_reduce_fusion.1), channel_id=1, source_target_pairs={{0,2},{1,3},{2,0},{3,1},{4,6},{5,7},{6,4},{7,5},{8,10},{9,11},{10,... | collective-permute-start | bytes 294920 | tf_op jit(solution)/shard_map/ppermute | solution.py:148
  51.7 8.8 %collective-permute-start = (bf16[64,768]{1,0:T(8,128)(2,1)S(1)}, bf16[64,768]{1,0:T(8,128)(2,1)S(1)}, u32[]{:S(2)}, u32[]{:S(2)}) collective-permute-start(bf16[64,768]{1,0:T(8,128)(2,1)S(1)} %select_reduce_fusion.1), channel_id=1, source_target_pairs={{0,1},{1,2},{2,3},{3,0},{4,5},{5,6},{6,7},{7,4},{8,9},{9,10},{10,1... | collective-permute-start | bytes 294920 | tf_op jit(solution)/shard_map/ppermute | solution.py:148
  51.7 8.8 %collective-permute-start.2 = (bf16[64,768]{1,0:T(8,128)(2,1)S(1)}, bf16[64,768]{1,0:T(8,128)(2,1)S(1)}, u32[]{:S(2)}, u32[]{:S(2)}) collective-permute-start(bf16[64,768]{1,0:T(8,128)(2,1)S(1)} %select_reduce_fusion.1), channel_id=1, source_target_pairs={{0,3},{1,0},{2,1},{3,2},{4,7},{5,4},{6,5},{7,6},{8,11},{9,8},{10,9... | collective-permute-start | bytes 294920 | tf_op jit(solution)/shard_map/ppermute | solution.py:148
  73.0 1.0 copy-start.5
  74.1 20.2 %collective-permute-start.4 = (bf16[64,768]{1,0:T(8,128)(2,1)S(1)}, bf16[64,768]{1,0:T(8,128)(2,1)}, u32[]{:S(2)}, u32[]{:S(2)}) collective-permute-start(bf16[64,768]{1,0:T(8,128)(2,1)S(1)} %select_reduce_fusion), channel_id=1, source_target_pairs={{0,2},{1,3},{2,0},{3,1},{4,6},{5,7},{6,4},{7,5},{8,10},{9,11},{10,... | collective-permute-start | bytes 294920 | tf_op jit(solution)/shard_map/ppermute | solution.py:148
  75.7 18.6 %collective-permute-start.3 = (bf16[64,768]{1,0:T(8,128)(2,1)S(1)}, bf16[64,768]{1,0:T(8,128)(2,1)}, u32[]{:S(2)}, u32[]{:S(2)}) collective-permute-start(bf16[64,768]{1,0:T(8,128)(2,1)S(1)} %select_reduce_fusion), channel_id=1, source_target_pairs={{0,1},{1,2},{2,3},{3,0},{4,5},{5,6},{6,7},{7,4},{8,9},{9,10},{10,1... | collective-permute-start | bytes 294920 | tf_op jit(solution)/shard_map/ppermute | solution.py:148
  75.7 18.6 %collective-permute-start.5 = (bf16[64,768]{1,0:T(8,128)(2,1)S(1)}, bf16[64,768]{1,0:T(8,128)(2,1)}, u32[]{:S(2)}, u32[]{:S(2)}) collective-permute-start(bf16[64,768]{1,0:T(8,128)(2,1)S(1)} %select_reduce_fusion), channel_id=1, source_target_pairs={{0,3},{1,0},{2,1},{3,2},{4,7},{5,4},{6,5},{7,6},{8,11},{9,8},{10,9... | collective-permute-start | bytes 294920 | tf_op jit(solution)/shard_map/ppermute | solution.py:148
  77.5 28.8 %all-to-all-start.2 = ((bf16[8,64,1024]{2,1,0:T(8,128)(2,1)}), bf16[8,64,1024]{2,1,0:T(8,128)(2,1)S(1)}, u32[]{:S(2)}, u32[]{:S(2)}) async-start(bf16[8,64,1024]{2,1,0:T(8,128)(2,1)} %bitcast.43), calls=%async_computation.2 | async-start | bytes 2097152 | tf_op jit(solution)/shard_map/all_to_all | solution.py:161
  81.1 11.1 %copy-start.6 = (bf16[8,64,1024]{2,1,0:T(8,128)(2,1)S(1)}, bf16[8,64,1024]{2,1,0:T(8,128)(2,1)}, u32[]{:S(2)}) copy-start(bf16[8,64,1024]{2,1,0:T(8,128)(2,1)} %copy-done.5) | copy-start | bytes 3145732
  92.2 3.3 %copy-start.7 = (bf16[768,1024]{1,0:T(8,128)(2,1)S(1)}, bf16[768,1024]{1,0:T(8,128)(2,1)}, u32[]{:S(2)}) copy-start(bf16[768,1024]{1,0:T(8,128)(2,1)} %param.11) | copy-start | bytes 4718596
  106.3 29.7 %all-to-all-start.3 = ((bf16[8,64,1024]{2,1,0:T(8,128)(2,1)}), bf16[8,64,1024]{2,1,0:T(8,128)(2,1)}, u32[]{:S(2)}, u32[]{:S(2)}) async-start(bf16[8,64,1024]{2,1,0:T(8,128)(2,1)} %bitcast.44), calls=%async_computation.3 | async-start | bytes 2097152 | tf_op jit(solution)/shard_map/all_to_all | solution.py:177
  110.7 1.2 copy-start.1
  114.9 21.1 %copy-start.2 = (f32[4,64,1024]{2,1,0:T(8,128)S(1)}, f32[4,64,1024]{2,1,0:T(8,128)}, u32[]{:S(2)}) copy-start(f32[4,64,1024]{2,1,0:T(8,128)} %moment_ref.3) | copy-start | bytes 3145732
Sparse Core Ops, SparseCore 0:
  9.6 53.1 all-gather.1
  65.3 58.1 reduce-scatter.1

commit v4 on v3

--- a/solution.py
+++ b/solution.py
@@ -63,7 +63,7 @@
 def lion(row, used, denom, incoming, moment):
     seq_count, rank, width = incoming.shape
     owned = moment.shape[0]
-    tile = min(256, width)
+    tile = min(128, width)
     block = pl.BlockSpec((owned, rank, tile), lambda j: (0, 0, j))
     shape = jax.ShapeDtypeStruct(moment.shape, jnp.float32)
     smem = pl.BlockSpec(memory_space=pltpu.SMEM)
@@ -138,30 +138,33 @@
     mask = (row_ids[None, :] >= first[:, None]) & (row_ids[None, :] < last[:, None])
     mask = mask[:, None, :]
 
-    def project(blocks, rows):
+    def project(blocks, rows, held=None):
         product = lax.dot_general(blocks, rows, contract_last, preferred_element_type=jnp.float32)
         part = jnp.sum(jnp.where(mask, product.reshape(seq_count, rank, row_count), 0.0), axis=0)
         part = part.astype(jnp.bfloat16)
+        if held is not None:
+            part, held = lax.optimization_barrier((part, held))
         total = part.astype(jnp.float32)
         for k in range(1, tp_count):
             order = [(i, (i + k) % tp_count) for i in range(tp_count)]
             total = total + lax.ppermute(part, "tp", order).astype(jnp.float32)
-        return total
+        return total, held
 
     def spread(values):
         wide = jnp.where(mask, values[None], jnp.zeros((), jnp.bfloat16))
         return wide.reshape(seq_count * rank, row_count)
 
-    low_grad = (adapter_scale * project(up, output_gradient)).astype(jnp.bfloat16)
+    low_grad = (adapter_scale * project(up, output_gradient)[0]).astype(jnp.bfloat16)
     spread_grad = spread(low_grad)
     part_down = jnp.dot(
         spread_grad, attention_output, preferred_element_type=jnp.float32
     ).astype(jnp.bfloat16)
-    part_down, gathered, down = lax.optimization_barrier((part_down, gathered, down))
+    part_down, down = lax.optimization_barrier((part_down, down))
     incoming_down = lax.all_to_all(
         part_down.reshape(seq_count, rank, width), "seq", split_axis=0, concat_axis=0, tiled=True
     )
-    low = project(down, attention_output).astype(jnp.bfloat16)
+    low_total, gathered = project(down, attention_output, gathered)
+    low = low_total.astype(jnp.bfloat16)
     spread_low = spread(low)
     part_up = (
         adapter_scale * jnp.dot(spread_low, output_gradient, preferred_element_type=jnp.float32)

time: 147 us -> 147 us (level)
  waiting for transfers between devices: 55.2 us -> 51.7 us
  Pallas kernels: 10.1 us -> 13.2 us
  starting transfers between devices: 25.5 us -> 24 us
    pallas_call x2, Pallas kernels: 6.92 us -> 10 us  [lion(): pl.pallas_call(functools.partial(lion_kernel, seq_count, owned), out_shap...]
    all_to_all x1, waiting for transfers between devices: 8.47 us -> 5.95 us  [local(): lax.all_to_all(part_up.reshape(seq_count, rank, width), 'seq', split_axis...]
    all_to_all x1, waiting for transfers between devices: 8.82 us -> 6.36 us  [local(): lax.all_to_all(part_down.reshape(seq_count, rank, width), 'seq', split_ax...]
    ppermute x6, starting transfers between devices: 6.67 us -> 5.16 us  [project(): total = total + lax.ppermute(part, 'tp', order).astype(jnp.float32)]
    reduce_scatter x1, waiting for transfers between devices: 8.68 us -> 10.2 us  [local(): lax.psum_scatter(base_terms, 'tp', scatter_dimension=1, tiled=True)]
  transfers between devices with their start and end apart: 12 -> 12, of which waited for: 7 -> 7; matrix products, arithmetic and copies ran while one was open for 27% -> 28% of each run, Pallas kernels for 4% -> 5%
where the time goes in v4:
time: 147 us; the launch traced here: 146 us
  waiting for transfers between devices  51.7 us (35%)
  matrix products  39.2 us (27%)
  starting transfers between devices  24 us (16%)
  between operations  14.2 us (10%)
  Pallas kernels  13.2 us (9%)
  local copies, waits for them, and re-layouts  2.66 us (2%)
    dot_general x1, matrix products, local(): jnp.dot(attention_output, output_weight, preferred_element_type=jnp.float32)  13.1 us
    all_to_all x1, waiting for transfers between devices, local(): up = lax.all_to_all(up_out, 'seq', split_axis=0, concat_axis=0, tiled=True)  11.1 us
    dot_general x1, matrix products, local(): lax.dot_general(gathered, output_weight, contract_last, preferred_element...  11 us
    all_to_all x1, waiting for transfers between devices, local(): lax.all_to_all(down_out, 'seq', split_axis=0, concat_axis=0, tiled=True)  10.4 us
    reduce_scatter x1, waiting for transfers between devices, local(): lax.psum_scatter(base_terms, 'tp', scatter_dimension=1, tiled=True)  10.2 us
    pallas_call x2, Pallas kernels, lion(): pl.pallas_call(functools.partial(lion_kernel, seq_count, owned), out_shap...  10 us
    all_to_all x1, starting transfers between devices, local(): up = lax.all_to_all(up_out, 'seq', split_axis=0, concat_axis=0, tiled=True)  7.28 us
    ppermute x6, waiting for transfers between devices, project(): total = total + lax.ppermute(part, 'tp', order).astype(jnp.float32)  7.02 us
  transfers between devices with their start and end apart: 12, of which 7 were waited for; matrix products, arithmetic and copies ran while one was open for 28% of the time, Pallas kernels for 5%

profile of v4, /device:TPU:0, one launch (start us, length us, event | category | flops | bytes accessed | tf_op | source)
XLA Modules:
  0.0 146.0 jit_solution(15231341399569402798)
XLA Ops:
  7.3 0.7 all-gather.2.cloned.1.call-update
  8.0 0.2 select_reduce_fusion.2
  8.4 1.6 %pick.2 = bf16[8,64,1024]{2,1,0:T(8,128)(2,1)} custom-call(s32[8]{0:T(128)S(1)} %get-tuple-element.43.which_ref.row_ref, bf16[4,64,1024]{2,1,0:T(8,128)(2,1)S(1)} %copy-done.3), custom_call_target="tpu_custom_call" | custom-call | bytes 2097152 | tf_op jit(solution)/shard_map/pick/pallas_call | solution.py:33
  10.0 7.3 %all-to-all-start = ((bf16[8,64,1024]{2,1,0:T(8,128)(2,1)}), bf16[8,64,1024]{2,1,0:T(8,128)(2,1)}, u32[]{:S(2)}, u32[]{:S(2)}) async-start(bf16[8,64,1024]{2,1,0:T(8,128)(2,1)} %pick.2), calls=%async_computation | async-start | bytes 2097152 | tf_op jit(solution)/shard_map/all_to_all | solution.py:116
  17.3 1.6 %pick.3 = bf16[8,64,1024]{2,1,0:T(8,128)(2,1)} custom-call(s32[8]{0:T(128)S(1)} %get-tuple-element.43.which_ref.row_ref, bf16[4,64,1024]{2,1,0:T(8,128)(2,1)S(1)} %copy-done.4), custom_call_target="tpu_custom_call" | custom-call | bytes 2097152 | tf_op jit(solution)/shard_map/pick/pallas_call | solution.py:33
  18.9 13.1 %convolution_convert_fusion = bf16[768,4096]{1,0:T(8,128)(2,1)} fusion(bf16[768,1024]{1,0:T(8,128)(2,1)S(1)} %copy-done, bf16[1024,4096]{1,0:T(8,128)(2,1)} %param.12), kind=kOutput, calls=%fused_computation | convolution fusion | flops 6445596672 | bytes 16252928 | tf_op jit(solution)/shard_map/dot_general | solution.py:117
  32.0 11.1 %all-to-all-done = bf16[8,64,1024]{2,1,0:T(8,128)(2,1)} async-done(((bf16[8,64,1024]{2,1,0:T(8,128)(2,1)}), bf16[8,64,1024]{2,1,0:T(8,128)(2,1)}, u32[]{:S(2)}, u32[]{:S(2)}) %all-to-all-start) | async-done | bytes 1048608 | tf_op jit(solution)/shard_map/all_to_all | solution.py:116
  43.1 0.2 dynamic-slice_reduce_fusion
  43.4 3.6 %all-to-all-start.1 = ((bf16[8,64,1024]{2,1,0:T(8,128)(2,1)}), bf16[8,64,1024]{2,1,0:T(8,128)(2,1)S(1)}, u32[]{:S(2)}, u32[]{:S(2)}) async-start(bf16[8,64,1024]{2,1,0:T(8,128)(2,1)} %pick.3), calls=%async_computation.1 | async-start | bytes 2097152 | tf_op jit(solution)/shard_map/all_to_all | solution.py:125
  47.3 2.8 %select_reduce_fusion.1 = bf16[64,768]{1,0:T(8,128)(2,1)S(1)} fusion(bf16[8,64,1024]{2,1,0:T(8,128)(2,1)} %all-to-all-done, bf16[768,1024]{1,0:T(8,128)(2,1)} %param.11, pred[8,768]{1,0:T(8,128)(4,1)S(1)} %fusion.6), kind=kOutput, calls=%fused_computation.9 | convolution fusion | flops 806043648 | bytes 2725888 | tf_op jit(solution)/shard_map/dot_general | solution.py:142
  50.1 1.6 %collective-permute-start.1 = (bf16[64,768]{1,0:T(8,128)(2,1)S(1)}, bf16[64,768]{1,0:T(8,128)(2,1)S(1)}, u32[]{:S(2)}, u32[]{:S(2)}) collective-permute-start(bf16[64,768]{1,0:T(8,128)(2,1)S(1)} %select_reduce_fusion.1), channel_id=1, source_target_pairs={{0,2},{1,3},{2,0},{3,1},{4,6},{5,7},{6,4},{7,5},{8,10},{9,11},{10,... | collective-permute-start | bytes 294920 | tf_op jit(solution)/shard_map/ppermute | solution.py:150
  51.7 1.7 %collective-permute-start.2 = (bf16[64,768]{1,0:T(8,128)(2,1)S(1)}, bf16[64,768]{1,0:T(8,128)(2,1)S(1)}, u32[]{:S(2)}, u32[]{:S(2)}) collective-permute-start(bf16[64,768]{1,0:T(8,128)(2,1)S(1)} %select_reduce_fusion.1), channel_id=1, source_target_pairs={{0,3},{1,0},{2,1},{3,2},{4,7},{5,4},{6,5},{7,6},{8,11},{9,8},{10,9... | collective-permute-start | bytes 294920 | tf_op jit(solution)/shard_map/ppermute | solution.py:150
  53.5 4.4 %collective-permute-done.1 = bf16[64,768]{1,0:T(8,128)(2,1)S(1)} collective-permute-done((bf16[64,768]{1,0:T(8,128)(2,1)S(1)}, bf16[64,768]{1,0:T(8,128)(2,1)S(1)}, u32[]{:S(2)}, u32[]{:S(2)}) %collective-permute-start.1) | collective-permute-done | bytes 98336 | tf_op jit(solution)/shard_map/ppermute | solution.py:150
  57.9 2.6 %collective-permute-done = bf16[64,768]{1,0:T(8,128)(2,1)S(1)} collective-permute-done((bf16[64,768]{1,0:T(8,128)(2,1)S(1)}, bf16[64,768]{1,0:T(8,128)(2,1)S(1)}, u32[]{:S(2)}, u32[]{:S(2)}) %collective-permute-start) | collective-permute-done | bytes 98336 | tf_op jit(solution)/shard_map/ppermute | solution.py:150
  60.6 2.0 %convolution_convert_fusion.1 = bf16[512,1024]{1,0:T(8,128)(2,1)} fusion(bf16[512,768]{1,0:T(8,128)(2,1)S(1)} %bitcast.40, bf16[768,1024]{1,0:T(8,128)(2,1)S(1)} %copy-done), kind=kOutput, calls=%fused_computation.10 | convolution fusion | flops 805830656 | bytes 3407872 | tf_op jit(solution)/shard_map/dot_general | solution.py:159
  62.6 10.4 %all-to-all-done.1 = bf16[8,64,1024]{2,1,0:T(8,128)(2,1)S(1)} async-done(((bf16[8,64,1024]{2,1,0:T(8,128)(2,1)}), bf16[8,64,1024]{2,1,0:T(8,128)(2,1)S(1)}, u32[]{:S(2)}, u32[]{:S(2)}) %all-to-all-start.1) | async-done | bytes 1048608 | tf_op jit(solution)/shard_map/all_to_all | solution.py:125
  73.0 1.0 copy-done.5
  73.9 3.6 %all-to-all-start.2 = ((bf16[8,64,1024]{2,1,0:T(8,128)(2,1)}), bf16[8,64,1024]{2,1,0:T(8,128)(2,1)S(1)}, u32[]{:S(2)}, u32[]{:S(2)}) async-start(bf16[8,64,1024]{2,1,0:T(8,128)(2,1)} %bitcast.43), calls=%async_computation.2 | async-start | bytes 2097152 | tf_op jit(solution)/shard_map/all_to_all | solution.py:163
  77.6 2.3 %fusion.11 = f32[512,768]{1,0:T(8,128)S(1)} fusion(bf16[512,1024]{1,0:T(8,128)(2,1)} %bitcast.38, bf16[768,1024]{1,0:T(8,128)(2,1)S(1)} %copy-done), kind=kOutput, calls=%fused_computation.45 | convolution fusion | flops 805306368 | bytes 4194304 | tf_op jit(solution)/shard_map/dot_general | solution.py:142
  80.1 0.9 collective-permute-start.5
  80.9 0.7 collective-permute-start.4
  81.9 11.0 %fusion.12 = f32[768,1024]{1,0:T(8,128)S(1)} fusion(bf16[768,4096]{1,0:T(8,128)(2,1)} %all-gather.2.cloned.1.call-done, bf16[1024,4096]{1,0:T(8,128)(2,1)} %param.12), kind=kOutput, calls=%fused_computation.46 | convolution fusion | flops 6442450944 | bytes 17825792 | tf_op jit(solution)/shard_map/dot_general | solution.py:172
  92.9 2.2 %add_convert_fusion = bf16[768,1024]{1,0:T(8,128)(2,1)} fusion(f32[768,1024]{1,0:T(8,128)S(1)} %fusion.12, bf16[512,768]{1,0:T(8,128)(2,1)S(1)} %bitcast.41, bf16[512,1024]{1,0:T(8,128)(2,1)S(1)} %bitcast.39), kind=kOutput, calls=%fused_computation.4 | convolution fusion | flops 806879232 | bytes 6553600 | tf_op jit(solution)/shard_map/dot_general | solution.py:177
  95.2 2.0 %multiply_convert_fusion = bf16[512,1024]{1,0:T(8,128)(2,1)} fusion(bf16[512,768]{1,0:T(8,128)(2,1)S(1)} %bitcast.45, bf16[768,1024]{1,0:T(8,128)(2,1)S(1)} %copy-done.7), kind=kOutput, calls=%fused_computation.5 | convolution fusion | flops 806354944 | bytes 3407872 | tf_op jit(solution)/shard_map/dot_general | solution.py:170
  97.2 6.4 %all-to-all-done.2.incoming_ref = bf16[8,64,1024]{2,1,0:T(8,128)(2,1)S(1)} async-done(((bf16[8,64,1024]{2,1,0:T(8,128)(2,1)}), bf16[8,64,1024]{2,1,0:T(8,128)(2,1)S(1)}, u32[]{:S(2)}, u32[]{:S(2)}) %all-to-all-start.2) | async-done | bytes 1048608 | tf_op jit(solution)/shard_map/all_to_all | solution.py:163
  103.5 4.2 %all-to-all-start.3 = ((bf16[8,64,1024]{2,1,0:T(8,128)(2,1)}), bf16[8,64,1024]{2,1,0:T(8,128)(2,1)}, u32[]{:S(2)}, u32[]{:S(2)}) async-start(bf16[8,64,1024]{2,1,0:T(8,128)(2,1)} %bitcast.44), calls=%async_computation.3 | async-start | bytes 2097152 | tf_op jit(solution)/shard_map/all_to_all | solution.py:180
  107.9 1.2 copy-done.1
  109.1 4.2 %lion.2 = (f32[4,64,1024]{2,1,0:T(8,128)}, f32[4,64,1024]{2,1,0:T(8,128)}) custom-call(s32[8]{0:T(128)S(1)} %get-tuple-element.43.which_ref.row_ref, f32[8]{0:T(128)S(1)} %get-tuple-element.40.used_ref, f32[4]{0:T(128)S(1)} %maximum_convert_fusion.scale_ref, bf16[8,64,1024]{2,1,0:T(8,128)(2,1)S(1)} %all-to-all-done.2.incoming_ref, f32[4,64,1024]{2,1,0:T(8,128)S(1)} %copy-done.1), custom_call_target="tpu_custom_call" | custom-call | flops 1048576 | bytes 4194304 | tf_op jit(solution)/shard_map/lion/pallas_call | solution.py:70
  113.4 10.2 %reduce-scatter.2.cloned.1.call-done = bf16[768,1024]{1,0:T(8,128)(2,1)} async-done(((bf16[768,4096]{1,0:T(8,128)(2,1)}), bf16[768,1024]{1,0:T(8,128)(2,1)}) %reduce-scatter.2.cloned.1.call-update) | async-done | bytes 1572880 | tf_op jit(solution)/shard_map/reduce_scatter | solution.py:121
  123.5 3.9 %fusion.1 = bf16[768,1024]{1,0:T(8,128)(2,1)} fusion(bf16[768,1024]{1,0:T(8,128)(2,1)} %reduce-scatter.2.cloned.1.call-done, bf16[8,64,1024]{2,1,0:T(8,128)(2,1)} %all-to-all-done, pred[8,768]{1,0:T(8,128)(4,1)S(1)} %fusion.6, bf16[64,768]{1,0:T(8,128)(2,1)S(1)} %add_convert_fusion.1), kind=kOutput, calls=%fused_computation.3 | convolution fusion | flops 808845312 | bytes 4298752 | tf_op jit(solution)/shard_map/dot_general | solution.py:187
  127.5 6.0 %all-to-all-done.3.incoming_ref = bf16[8,64,1024]{2,1,0:T(8,128)(2,1)} async-done(((bf16[8,64,1024]{2,1,0:T(8,128)(2,1)}), bf16[8,64,1024]{2,1,0:T(8,128)(2,1)}, u32[]{:S(2)}, u32[]{:S(2)}) %all-to-all-start.3) | async-done | bytes 1048608 | tf_op jit(solution)/shard_map/all_to_all | solution.py:180
  133.4 5.8 %lion.3 = (f32[4,64,1024]{2,1,0:T(8,128)}, f32[4,64,1024]{2,1,0:T(8,128)}) custom-call(s32[8]{0:T(128)S(1)} %get-tuple-element.43.which_ref.row_ref, f32[8]{0:T(128)S(1)} %get-tuple-element.40.used_ref, f32[4]{0:T(128)S(1)} %maximum_convert_fusion.scale_ref, bf16[8,64,1024]{2,1,0:T(8,128)(2,1)} %all-to-all-done.3.incoming_ref, f32[4,64,1024]{2,1,0:T(8,128)S(1)} %copy-done.2), custom_call_target="tpu_custom_call" | custom-call | flops 1048576 | bytes 4194304 | tf_op jit(solution)/shard_map/lion/pallas_call | solution.py:70
  (44 shorter events, 1.4 us)
Async XLA Ops:
  7.2 11.7 %copy-start = (bf16[768,1024]{1,0:T(8,128)(2,1)S(1)}, bf16[768,1024]{1,0:T(8,128)(2,1)}, u32[]{:S(2)}) copy-start(bf16[768,1024]{1,0:T(8,128)(2,1)} %param.10) | copy-start | bytes 4718596
  7.2 0.8 copy-start.9
  7.2 0.8 copy-start.10
  7.2 1.2 copy-start.3
  7.2 72.8 %all-gather.2.cloned.1.call-start = ((), (), s32[]{:S(2)}) async-start(), calls=%async_computation.5 | async-start | bytes 7864320 | tf_op jit(solution)/shard_map/all_gather | solution.py:128
  8.4 8.9 %copy-start.4 = (bf16[4,64,1024]{2,1,0:T(8,128)(2,1)S(1)}, bf16[4,64,1024]{2,1,0:T(8,128)(2,1)}, u32[]{:S(2)}) copy-start(bf16[4,64,1024]{2,1,0:T(8,128)(2,1)} %in_ref.3) | copy-start | bytes 1572868
  10.0 33.2 %all-to-all-start = ((bf16[8,64,1024]{2,1,0:T(8,128)(2,1)}), bf16[8,64,1024]{2,1,0:T(8,128)(2,1)}, u32[]{:S(2)}, u32[]{:S(2)}) async-start(bf16[8,64,1024]{2,1,0:T(8,128)(2,1)} %pick.2), calls=%async_computation | async-start | bytes 2097152 | tf_op jit(solution)/shard_map/all_to_all | solution.py:116
  17.2 106.3 %reduce-scatter.2.cloned.1.call-start = ((), (), s32[]{:S(2)}) async-start(), calls=%async_computation.6 | async-start | bytes 7864320 | tf_op jit(solution)/shard_map/reduce_scatter | solution.py:121
  32.0 11.1 %copy-start.8 = (s32[8,4]{0,1:T(4,128)S(1)}, s32[8,4]{0,1:T(4,128)}, u32[]{:S(2)}) copy-start(s32[8,4]{0,1:T(4,128)} %param.19) | copy-start | bytes 388
  43.4 29.5 %all-to-all-start.1 = ((bf16[8,64,1024]{2,1,0:T(8,128)(2,1)}), bf16[8,64,1024]{2,1,0:T(8,128)(2,1)S(1)}, u32[]{:S(2)}, u32[]{:S(2)}) async-start(bf16[8,64,1024]{2,1,0:T(8,128)(2,1)} %pick.3), calls=%async_computation.1 | async-start | bytes 2097152 | tf_op jit(solution)/shard_map/all_to_all | solution.py:125
  50.1 7.8 %collective-permute-start.1 = (bf16[64,768]{1,0:T(8,128)(2,1)S(1)}, bf16[64,768]{1,0:T(8,128)(2,1)S(1)}, u32[]{:S(2)}, u32[]{:S(2)}) collective-permute-start(bf16[64,768]{1,0:T(8,128)(2,1)S(1)} %select_reduce_fusion.1), channel_id=1, source_target_pairs={{0,2},{1,3},{2,0},{3,1},{4,6},{5,7},{6,4},{7,5},{8,10},{9,11},{10,... | collective-permute-start | bytes 294920 | tf_op jit(solution)/shard_map/ppermute | solution.py:150
  51.7 8.8 %collective-permute-start = (bf16[64,768]{1,0:T(8,128)(2,1)S(1)}, bf16[64,768]{1,0:T(8,128)(2,1)S(1)}, u32[]{:S(2)}, u32[]{:S(2)}) collective-permute-start(bf16[64,768]{1,0:T(8,128)(2,1)S(1)} %select_reduce_fusion.1), channel_id=1, source_target_pairs={{0,1},{1,2},{2,3},{3,0},{4,5},{5,6},{6,7},{7,4},{8,9},{9,10},{10,1... | collective-permute-start | bytes 294920 | tf_op jit(solution)/shard_map/ppermute | solution.py:150
  51.7 8.8 %collective-permute-start.2 = (bf16[64,768]{1,0:T(8,128)(2,1)S(1)}, bf16[64,768]{1,0:T(8,128)(2,1)S(1)}, u32[]{:S(2)}, u32[]{:S(2)}) collective-permute-start(bf16[64,768]{1,0:T(8,128)(2,1)S(1)} %select_reduce_fusion.1), channel_id=1, source_target_pairs={{0,3},{1,0},{2,1},{3,2},{4,7},{5,4},{6,5},{7,6},{8,11},{9,8},{10,9... | collective-permute-start | bytes 294920 | tf_op jit(solution)/shard_map/ppermute | solution.py:150
  73.0 1.0 copy-start.5
  73.9 29.6 %all-to-all-start.2 = ((bf16[8,64,1024]{2,1,0:T(8,128)(2,1)}), bf16[8,64,1024]{2,1,0:T(8,128)(2,1)S(1)}, u32[]{:S(2)}, u32[]{:S(2)}) async-start(bf16[8,64,1024]{2,1,0:T(8,128)(2,1)} %bitcast.43), calls=%async_computation.2 | async-start | bytes 2097152 | tf_op jit(solution)/shard_map/all_to_all | solution.py:163
  80.0 12.8 %copy-start.6 = (bf16[8,64,1024]{2,1,0:T(8,128)(2,1)S(1)}, bf16[8,64,1024]{2,1,0:T(8,128)(2,1)}, u32[]{:S(2)}) copy-start(bf16[8,64,1024]{2,1,0:T(8,128)(2,1)} %copy-done.5) | copy-start | bytes 3145732
  80.1 15.0 %collective-permute-start.5 = (bf16[64,768]{1,0:T(8,128)(2,1)S(1)}, bf16[64,768]{1,0:T(8,128)(2,1)S(1)}, u32[]{:S(2)}, u32[]{:S(2)}) collective-permute-start(bf16[64,768]{1,0:T(8,128)(2,1)S(1)} %select_reduce_fusion), channel_id=1, source_target_pairs={{0,3},{1,0},{2,1},{3,2},{4,7},{5,4},{6,5},{7,6},{8,11},{9,8},{10,9... | collective-permute-start | bytes 294920 | tf_op jit(solution)/shard_map/ppermute | solution.py:150
  80.9 14.1 %collective-permute-start.4 = (bf16[64,768]{1,0:T(8,128)(2,1)S(1)}, bf16[64,768]{1,0:T(8,128)(2,1)S(1)}, u32[]{:S(2)}, u32[]{:S(2)}) collective-permute-start(bf16[64,768]{1,0:T(8,128)(2,1)S(1)} %select_reduce_fusion), channel_id=1, source_target_pairs={{0,2},{1,3},{2,0},{3,1},{4,6},{5,7},{6,4},{7,5},{8,10},{9,11},{10,... | collective-permute-start | bytes 294920 | tf_op jit(solution)/shard_map/ppermute | solution.py:150
  81.7 13.4 %collective-permute-start.3 = (bf16[64,768]{1,0:T(8,128)(2,1)S(1)}, bf16[64,768]{1,0:T(8,128)(2,1)S(1)}, u32[]{:S(2)}, u32[]{:S(2)}) collective-permute-start(bf16[64,768]{1,0:T(8,128)(2,1)S(1)} %select_reduce_fusion), channel_id=1, source_target_pairs={{0,1},{1,2},{2,3},{3,0},{4,5},{5,6},{6,7},{7,4},{8,9},{9,10},{10,1... | collective-permute-start | bytes 294920 | tf_op jit(solution)/shard_map/ppermute | solution.py:150
  92.8 2.3 %copy-start.7 = (bf16[768,1024]{1,0:T(8,128)(2,1)S(1)}, bf16[768,1024]{1,0:T(8,128)(2,1)}, u32[]{:S(2)}) copy-start(bf16[768,1024]{1,0:T(8,128)(2,1)} %param.11) | copy-start | bytes 4718596
  103.5 29.9 %all-to-all-start.3 = ((bf16[8,64,1024]{2,1,0:T(8,128)(2,1)}), bf16[8,64,1024]{2,1,0:T(8,128)(2,1)}, u32[]{:S(2)}, u32[]{:S(2)}) async-start(bf16[8,64,1024]{2,1,0:T(8,128)(2,1)} %bitcast.44), calls=%async_computation.3 | async-start | bytes 2097152 | tf_op jit(solution)/shard_map/all_to_all | solution.py:180
  107.9 1.2 copy-start.1
  113.4 20.0 %copy-start.2 = (f32[4,64,1024]{2,1,0:T(8,128)S(1)}, f32[4,64,1024]{2,1,0:T(8,128)}, u32[]{:S(2)}) copy-start(f32[4,64,1024]{2,1,0:T(8,128)} %moment_ref.3) | copy-start | bytes 3145732
Sparse Core Ops, SparseCore 0:
  9.6 53.1 all-gather.1
  65.3 58.1 reduce-scatter.1
